TPU v7x, 32 devices: a whole 2x2x4 slice. The times are simulated.
32 devices in a mesh: chan: 4 (over z), tm: 2 (over y), row: 4 (over x, core).
Axes of the slice: x: 2, y: 2, z: 4, core: 2. Of those that a mesh axis runs over, the one named last changes fastest.
Arguments:
- samples: bfloat16 [8, 4096, 4096], P(('tm', 'row'), None, 'chan'), may hold values from -6 to 6
- channel_index: int32 [16], replicated, may hold values from 1 to 2047
- gain_real: float32 [16, 4096], P(None, 'chan'), may hold values from -4 to 4
- gain_imag: float32 [16, 4096], P(None, 'chan'), may hold values from -4 to 4
- flags: int32 [2048], P('chan'), may hold values 0 or 1
Outputs:
- visibility: bfloat16 [2, 16, 4096, 4096], P(None, 'chan', 'row', 'tm')
Inputs may be any that keep to these rules, and one draw needn't show every extreme that they name: `channel_index`: channel numbers, not necessarily distinct.
All inputs are finite; a program needn't handle non-finite values. No bound on the sum of `flags` on one device may be relied on, other than what follows from the above.
Results may differ from a plain program's by a relative error of at most 0.0056.
Values may be sent and summed in bfloat16 or wider, within the bound.
No kernel may reach another device: no remote copies, remote signals or barrier semaphores. Data moves between devices by JAX's collectives and lax.ppermute only.
A program may use at most 256 MiB of HBM per device.

v0:
```python
import math

import jax
import jax.numpy as jnp
from jax import lax
from jax.sharding import PartitionSpec as P

P_SIZE = 4096
TAPS = 4
CHANNELS = 16


def shifted(value, axis, by):
    peers = lax.axis_size(axis)
    pairs = [(i, i + by) for i in range(peers) if 0 <= i + by < peers]
    return lax.ppermute(value, axis, pairs)


def filter_taps():
    sample_index = jnp.arange(TAPS * P_SIZE, dtype=jnp.int32).astype(jnp.float32)
    centered = (sample_index + 0.5 - TAPS * P_SIZE / 2) / P_SIZE
    hann_taper = 0.5 - 0.5 * jnp.cos(2.0 * math.pi * (sample_index + 0.5) / (TAPS * P_SIZE))
    return (jnp.sinc(centered) * hann_taper).reshape(TAPS, P_SIZE)


def dft_table(channel_index):
    points = jnp.arange(P_SIZE, dtype=jnp.int32)
    phase_index = channel_index[:, None] * points[None, :] % P_SIZE
    angles = 2.0 * math.pi * phase_index.astype(jnp.float32) / P_SIZE
    scale = 1.0 / math.sqrt(P_SIZE)
    return jnp.concatenate([jnp.cos(angles) * scale, -jnp.sin(angles) * scale], 0)


def local(samples, channel_index, gain_real, gain_imag, flags):
    frames_dev = samples.shape[0]
    filters = filter_taps()
    table = dft_table(channel_index)
    shifts_needed = (TAPS - 2) // frames_dev + 1
    tables = filters[:, None, :] * table[None]
    partials = jnp.einsum(
        "kcp,fpi->kfci", tables, samples.astype(jnp.float32), precision=lax.Precision.HIGHEST
    )
    length = (shifts_needed + 1) * frames_dev
    local_sum = None
    for tap_number in range(TAPS):
        before = TAPS - 1 - tap_number
        placed = jnp.pad(
            partials[tap_number], ((before, length - frames_dev - before), (0, 0), (0, 0))
        )
        local_sum = placed if local_sum is None else local_sum + placed
    spectra = local_sum[0:frames_dev]
    for offset in range(1, shifts_needed + 1):
        spectra = spectra + shifted(
            local_sum[offset * frames_dev : (offset + 1) * frames_dev], ("tm", "row"), offset
        )
    spec_re = spectra[:, :CHANNELS]
    spec_im = spectra[:, CHANNELS:]
    usable = jnp.repeat(flags, 2).astype(jnp.float32)
    volt_re = (usable * (gain_real * spec_re - gain_imag * spec_im)).astype(jnp.bfloat16)
    volt_im = (usable * (gain_real * spec_im + gain_imag * spec_re)).astype(jnp.bfloat16)
    turned = jnp.stack([volt_re, volt_im], 1)
    turned = lax.all_to_all(turned, "chan", split_axis=2, concat_axis=3, tiled=True)
    inputs_total = turned.shape[3]
    row_count = inputs_total // lax.axis_size("row")
    col_count = inputs_total // lax.axis_size("tm")
    whole_panel = lax.all_gather(turned, "row", axis=0, tiled=True)
    whole_panel = lax.all_gather(whole_panel, "tm", axis=0, tiled=True)
    frames_total = whole_panel.shape[0]
    row_start = lax.axis_index("row") * row_count
    col_start = lax.axis_index("tm") * col_count
    panel_re = whole_panel[:, 0]
    panel_im = whole_panel[:, 1]
    rows_re = lax.dynamic_slice_in_dim(panel_re, row_start, row_count, 2)
    rows_im = lax.dynamic_slice_in_dim(panel_im, row_start, row_count, 2)
    cols_re = lax.dynamic_slice_in_dim(panel_re, col_start, col_count, 2)
    cols_im = lax.dynamic_slice_in_dim(panel_im, col_start, col_count, 2)
    left_side = jnp.concatenate([rows_re, rows_im], 0)
    right_side = jnp.concatenate(
        [jnp.concatenate([cols_re, -cols_im], 2), jnp.concatenate([cols_im, cols_re], 2)], 0
    )
    product = jnp.einsum("fcr,fcq->crq", left_side, right_side, preferred_element_type=jnp.float32)
    result = jnp.stack([product[:, :, :col_count], product[:, :, col_count:]], 0) / frames_total
    return result.astype(jnp.bfloat16)


def solution(mesh):
    in_specs = (P(("tm", "row"), None, "chan"), P(), P(None, "chan"), P(None, "chan"), P("chan"))
    out_specs = P(None, "chan", "row", "tm")
    return jax.shard_map(local, mesh=mesh, in_specs=in_specs, out_specs=out_specs, check_vma=False)
```

profile of v0, /device:TPU:0, one launch (start us, length us, event | category | flops | bytes accessed | tf_op | source)
XLA Modules:
  0.0 149.5 jit_solution(10176154775488916355)
XLA Ops:
  0.0 0.6 fusion.30
  0.6 1.8 %cosine_multiply_fusion = (f32[16,4096]{1,0:T(8,128)S(1)}, f32[16,4096]{1,0:T(8,128)S(1)}) fusion(s32[16]{0:T(128)} %param.6), kind=kLoop, calls=%fused_computation.26 | loop fusion | flops 1114112 | bytes 524352 | tf_op jit(solution)/shard_map/mul | solution.py:31
  2.4 6.1 %fusion.1 = f32[4,32,1024]{2,1,0:T(8,128)S(1)} fusion(bf16[1,4096,1024]{2,1,0:T(8,128)(2,1)} %param.5, f32[32,4096]{1,0:T(8,128)S(1)} %pad_maximum_fusion, f32[4,4096]{1,0:T(4,128)S(1)} %fusion.30), kind=kOutput, calls=%fused_computation.4 | convolution fusion | flops 6442975232 | bytes 9502720 | tf_op jit(solution)/shard_map/kcp,fpi->kfci/dot_general | solution.py:40
  8.7 2.4 %collective-permute-start = (f32[1,32,1024]{2,1,0:T(8,128)S(1)}, f32[1,32,1024]{2,1,0:T(8,128)S(1)}, u32[]{:S(2)}, u32[]{:S(2)}) collective-permute-start(f32[1,32,1024]{2,1,0:T(8,128)S(1)} %get-tuple-element.9), channel_id=1, source_target_pairs={{0,1},{1,2},{2,3},{3,4},{4,5},{5,6},{6,7},{8,9},{9,10},{10,11},{11... | collective-permute-start | bytes 393224 | tf_op jit(solution)/shard_map/ppermute | solution.py:16
  11.1 5.6 %collective-permute-start.2 = (f32[1,32,1024]{2,1,0:T(8,128)S(1)}, f32[1,32,1024]{2,1,0:T(8,128)S(1)}, u32[]{:S(2)}, u32[]{:S(2)}) collective-permute-start(f32[1,32,1024]{2,1,0:T(8,128)S(1)} %get-tuple-element.10), channel_id=1, source_target_pairs={{0,3},{1,4},{2,5},{3,6},{4,7},{8,11},{9,12},{10,13},{11,14},{12,15... | collective-permute-start | bytes 393224 | tf_op jit(solution)/shard_map/ppermute | solution.py:16
  16.7 3.4 %collective-permute-start.1 = (f32[1,32,1024]{2,1,0:T(8,128)S(1)}, f32[1,32,1024]{2,1,0:T(8,128)S(1)}, u32[]{:S(2)}, u32[]{:S(2)}) collective-permute-start(f32[1,32,1024]{2,1,0:T(8,128)S(1)} %get-tuple-element.11), channel_id=1, source_target_pairs={{0,2},{1,3},{2,4},{3,5},{4,6},{5,7},{8,10},{9,11},{10,12},{11,13},... | collective-permute-start | bytes 393224 | tf_op jit(solution)/shard_map/ppermute | solution.py:16
  20.1 0.7 convert_element_type.44
  20.8 0.1 broadcast_in_dim.11
  20.9 0.2 convert_element_type.45
  21.1 0.0 collective-permute-done
  21.1 0.0 collective-permute-done.2
  21.1 1.5 collective-permute-done.1
  22.6 0.9 fusion.43
  23.5 0.7 copy.20
  24.2 4.9 %all-to-all-start = ((bf16[1,2,16,1024]{3,1,0,2:T(2,128)(2,1)}), bf16[1,2,16,1024]{3,1,0,2:T(2,128)(2,1)S(1)}, u32[]{:S(2)}, u32[]{:S(2)}) async-start(bf16[1,2,16,1024]{3,1,0,2:T(2,128)(2,1)} %copy.20), calls=%async_computation | async-start | bytes 131072 | tf_op jit(solution)/shard_map/all_to_all | solution.py:62
  29.1 5.7 %all-to-all-done = bf16[1,2,16,1024]{3,1,0,2:T(2,128)(2,1)S(1)} async-done(((bf16[1,2,16,1024]{3,1,0,2:T(2,128)(2,1)}), bf16[1,2,16,1024]{3,1,0,2:T(2,128)(2,1)S(1)}, u32[]{:S(2)}, u32[]{:S(2)}) %all-to-all-start) | async-done | bytes 65568 | tf_op jit(solution)/shard_map/all_to_all | solution.py:62
  34.9 0.1 copy.37
  34.9 0.1 all_to_all.16
  35.0 6.7 %all_gather.6 = bf16[4,2,4,4096]{3,2,1,0:T(4,128)(2,1)S(1)} all-gather(bf16[1,2,4,4096]{3,2,1,0:T(4,128)(2,1)S(1)} %all_to_all.16), channel_id=1, replica_groups=mesh['chan'=4,'tm'=2,'row'=4] {'row'}, dimensions={0}, use_global_device_ids=true | all-gather | bytes 327680 | tf_op jit(solution)/shard_map/all_gather | solution.py:66
  41.7 9.3 %all_gather.7 = bf16[8,2,4,4096]{3,2,1,0:T(4,128)(2,1)S(1)} all-gather(bf16[4,2,4,4096]{3,2,1,0:T(4,128)(2,1)S(1)} %all_gather.6), channel_id=1, replica_groups=mesh['chan'=4,'tm'=2,'row'=4] {'tm'}, dimensions={0}, use_global_device_ids=true | all-gather | bytes 786432 | tf_op jit(solution)/shard_map/all_gather | solution.py:67
  51.0 0.2 fusion.46
  51.2 0.1 constant_dynamic-slice_fusion
  51.3 0.1 fusion.45
  51.4 0.1 copy.33
  51.5 0.1 constant_dynamic-slice_fusion.2
  51.6 0.1 copy.34
  51.7 23.1 %fusion.6 = f32[4,1024,4096]{2,1,0:T(8,128)} fusion(bf16[8,4,2048]{2,0,1:T(8,128)(2,1)S(1)} %bitcast.80, bf16[8,4,2048]{2,0,1:T(8,128)(2,1)S(1)} %bitcast.79, bf16[8,4,2048]{2,0,1:T(8,128)(2,1)S(1)} %fusion.45, bf16[8,4,1024]{2,0,1:T(8,128)(2,1)S(1)} %bitcast.83, bf16[8,4,1024]{2,0,1:T(8,128)(2,1)S(1)} %bitcast.84), kind=kOutput, calls=%fused_computation.10 | convolution fusion | flops 539230208 | bytes 67633152 | tf_op jit(solution)/shard_map/fcr,fcq->crq/dot_general | solution.py:81
  74.9 42.0 %slice_bitcast_fusion.1 = (f32[1,4,1024,2048]{3,2,1,0:T(8,128)}, f32[1,4,1024,2048]{3,2,1,0:T(8,128)}) fusion(f32[4,1024,4096]{2,1,0:T(8,128)} %fusion.6), kind=kLoop, calls=%fused_computation.3 | loop fusion | bytes 134217728 | tf_op jit(solution)/shard_map/stack | solution.py:82
  116.8 32.7 %fusion = bf16[2,4,1024,2048]{3,2,1,0:T(8,128)(2,1)} fusion(f32[1,4,1024,2048]{3,2,1,0:T(8,128)} %get-tuple-element.6, f32[1,4,1024,2048]{3,2,1,0:T(8,128)} %get-tuple-element.5), kind=kLoop, calls=%fused_computation.1 | loop fusion | flops 50331648 | bytes 100663296 | tf_op jit(solution)/shard_map/convert_element_type | solution.py:83
  (9 shorter events, 0.2 us)
Async XLA Ops:
  8.7 12.4 %collective-permute-start = (f32[1,32,1024]{2,1,0:T(8,128)S(1)}, f32[1,32,1024]{2,1,0:T(8,128)S(1)}, u32[]{:S(2)}, u32[]{:S(2)}) collective-permute-start(f32[1,32,1024]{2,1,0:T(8,128)S(1)} %get-tuple-element.9), channel_id=1, source_target_pairs={{0,1},{1,2},{2,3},{3,4},{4,5},{5,6},{6,7},{8,9},{9,10},{10,11},{11... | collective-permute-start | bytes 393224 | tf_op jit(solution)/shard_map/ppermute | solution.py:16
  11.1 10.0 %collective-permute-start.2 = (f32[1,32,1024]{2,1,0:T(8,128)S(1)}, f32[1,32,1024]{2,1,0:T(8,128)S(1)}, u32[]{:S(2)}, u32[]{:S(2)}) collective-permute-start(f32[1,32,1024]{2,1,0:T(8,128)S(1)} %get-tuple-element.10), channel_id=1, source_target_pairs={{0,3},{1,4},{2,5},{3,6},{4,7},{8,11},{9,12},{10,13},{11,14},{12,15... | collective-permute-start | bytes 393224 | tf_op jit(solution)/shard_map/ppermute | solution.py:16
  16.7 5.9 %collective-permute-start.1 = (f32[1,32,1024]{2,1,0:T(8,128)S(1)}, f32[1,32,1024]{2,1,0:T(8,128)S(1)}, u32[]{:S(2)}, u32[]{:S(2)}) collective-permute-start(f32[1,32,1024]{2,1,0:T(8,128)S(1)} %get-tuple-element.11), channel_id=1, source_target_pairs={{0,2},{1,3},{2,4},{3,5},{4,6},{5,7},{8,10},{9,11},{10,12},{11,13},... | collective-permute-start | bytes 393224 | tf_op jit(solution)/shard_map/ppermute | solution.py:16
  24.2 10.6 %all-to-all-start = ((bf16[1,2,16,1024]{3,1,0,2:T(2,128)(2,1)}), bf16[1,2,16,1024]{3,1,0,2:T(2,128)(2,1)S(1)}, u32[]{:S(2)}, u32[]{:S(2)}) async-start(bf16[1,2,16,1024]{3,1,0,2:T(2,128)(2,1)} %copy.20), calls=%async_computation | async-start | bytes 131072 | tf_op jit(solution)/shard_map/all_to_all | solution.py:62
where the time goes:
time: 150 us
  local copies, waits for them, and re-layouts  43.7 us (29%)
  other arithmetic  36.9 us (25%)
  matrix products  29.2 us (19%)
  starting transfers between devices  16.3 us (11%)
  blocking collectives  16 us (11%)
  waiting for transfers between devices  7.24 us (5%)
    another operation x1, local copies, waits for them, and re-layouts, local(): jnp.stack([product[:, :, :col_count], product[:, :, col_count:]], 0)  42 us
    convert_element_type x1, other arithmetic, local(): return result.astype(jnp.bfloat16)  32.7 us
    dot_general x1, matrix products, local(): jnp.einsum('fcr,fcq->crq', left_side, right_side, preferred_element_type=...  23.1 us
    ppermute x3, starting transfers between devices, shifted(): return lax.ppermute(value, axis, pairs)  11.4 us
    all_gather x1, blocking collectives, local(): whole_panel = lax.all_gather(whole_panel, 'tm', axis=0, tiled=True)  9.32 us
    all_gather x1, blocking collectives, local(): whole_panel = lax.all_gather(turned, 'row', axis=0, tiled=True)  6.7 us
    dot_general x1, matrix products, local(): jnp.einsum('kcp,fpi->kfci', tables, samples.astype(jnp.float32), precisio...  6.09 us
    all_to_all x1, waiting for transfers between devices, local(): lax.all_to_all(turned, 'chan', split_axis=2, concat_axis=3, tiled=True)  5.74 us
  transfers between devices with their start and end apart: 4, of which 2 were waited for; matrix products, arithmetic and copies ran while one was open for 1% of the time, Pallas kernels for 0%

commit v1 on v0

v1 whole, which is shorter than its diff:
```python
import functools
import math

import jax
import jax.numpy as jnp
from jax import lax
from jax.experimental import pallas as pl
from jax.experimental.pallas import tpu as pltpu
from jax.sharding import PartitionSpec as P

TAPS = 4
LANES = 128
PAIR_TAPS = (1, 2)
SPLITS = 8
TILE = 512
VMEM_BYTES = 48 << 20
FRAME_AXES = ("tm", "row")

IN_VMEM = pl.BlockSpec(memory_space=pltpu.VMEM)
IN_HBM = pl.BlockSpec(memory_space=pltpu.HBM)


def in_hbm(*arrays):
    return [pltpu.with_memory_space_constraint(a, pltpu.HBM) for a in arrays]


def shifted(value, axis, by, wrap):
    peers = lax.axis_size(axis)
    pairs = [(i, (i + by) % peers) for i in range(peers) if wrap or i + by < peers]
    return lax.ppermute(value, axis, pairs)


def sine_quarter(x):
    y = x * x
    acc = 1.0 / 6227020800.0
    for k in (-1.0 / 39916800.0, 1.0 / 362880.0, -1.0 / 5040.0, 1.0 / 120.0, -1.0 / 6.0, 1.0):
        acc = acc * y + k
    return acc * x


def turn(m, quarter):
    q = (m + quarter // 2) >> (quarter.bit_length() - 1)
    r = (m - q * quarter).astype(jnp.float32) * (math.pi / 2 / quarter)
    y = r * r
    cos = ((((-1.0 / 3628800.0 * y + 1.0 / 40320.0) * y - 1.0 / 720.0) * y + 1.0 / 24.0) * y - 0.5) * y + 1.0
    sin = ((((1.0 / 362880.0 * y - 1.0 / 5040.0) * y + 1.0 / 120.0) * y - 1.0 / 6.0) * y + 1.0) * r
    odd = (q & 1) == 1
    first = jnp.where(odd, sin, cos)
    second = jnp.where(odd, cos, sin)
    return jnp.where(((q + 1) & 2) != 0, -first, first), jnp.where((q & 2) != 0, -second, second)


def front_body(
    index_hbm, samples_ref, gr_hbm, gi_hbm, flags_hbm,
    own_ref, one_ref, two_ref, three_ref,
    index_ref, gr_ref, gi_ref, flags_ref, block_ref, filter_ref, table_ref, acc_ref, sems, small_sems,
    *, groups,
):
    points, width = block_ref.shape
    channels = gr_ref.shape[0]
    cg = channels // groups
    rows = 2 * channels
    quarter = points // 4
    index_copy = pltpu.make_async_copy(index_hbm, index_ref, small_sems.at[0])
    index_copy.start()
    part = points // SPLITS
    fetches = [
        pltpu.make_async_copy(
            samples_ref.at[0, pl.ds(i * part, part), :], block_ref.at[pl.ds(i * part, part), :], sems.at[i]
        )
        for i in range(SPLITS)
    ]
    for copy in fetches:
        copy.start()
    others = [
        pltpu.make_async_copy(src, dst, small_sems.at[1 + i])
        for i, (src, dst) in enumerate(((gr_hbm, gr_ref), (gi_hbm, gi_ref), (flags_hbm, flags_ref)))
    ]
    for copy in others:
        copy.start()

    spans = points // LANES
    at = lax.broadcasted_iota(jnp.int32, (spans, LANES), 0) * LANES
    at = at + lax.broadcasted_iota(jnp.int32, (spans, LANES), 1)
    u = (at.astype(jnp.float32) + 0.5) * (1.0 / points)
    sn = sine_quarter(u * (math.pi / 2))
    cs = sine_quarter((1.0 - u) * (math.pi / 2))
    sp = 2.0 * sn * cs * (1.0 / math.pi / math.sqrt(points))
    filter_ref[0] = sp / (u - 2.0) * (0.5 - 0.5 * cs)
    filter_ref[1] = -sp / (u - 1.0) * (0.5 + 0.5 * sn)
    filter_ref[2] = sp / u * (0.5 + 0.5 * cs)
    filter_ref[3] = -sp / (u + 1.0) * (0.5 - 0.5 * sn)

    rho = lax.broadcasted_iota(jnp.int32, (rows, LANES), 0)
    lane = lax.broadcasted_iota(jnp.int32, (rows, LANES), 1)
    chan = lax.div(rho, 2 * cg) * cg + lax.rem(rho, cg)
    imag = jnp.where(lax.rem(rho, 2 * cg) >= cg, quarter, 0)
    index_copy.wait()
    index = jnp.zeros((rows, LANES), jnp.int32)
    for c in range(channels):
        index = jnp.where(chan == c, index_ref[c], index)
    cos_a, sin_a = turn(index * lane + imag, quarter)
    cos_b, sin_b = turn(index * lane * LANES, quarter)
    for a in range(spans):
        v = cos_a * cos_b[:, a : a + 1] - sin_a * sin_b[:, a : a + 1]
        cols = slice(a * LANES, (a + 1) * LANES)
        for k in range(TAPS):
            t = filter_ref[k, a : a + 1, :] * v
            high = t.astype(jnp.bfloat16)
            table_ref[k * rows : (k + 1) * rows, cols] = high
            if k in PAIR_TAPS:
                i = TAPS + PAIR_TAPS.index(k)
                table_ref[i * rows : (i + 1) * rows, cols] = (t - high.astype(jnp.float32)).astype(jnp.bfloat16)
    for i, copy in enumerate(fetches):
        copy.wait()
        span = slice(i * part, (i + 1) * part)
        product = jnp.dot(table_ref[:, span], block_ref[span, :], preferred_element_type=jnp.float32)
        acc_ref[...] = product if i == 0 else acc_ref[...] + product

    for copy in others:
        copy.wait()
    row = lax.broadcasted_iota(jnp.int32, (LANES, 2 * LANES), 0)
    col = lax.broadcasted_iota(jnp.int32, (LANES, 2 * LANES), 1)
    spread = jnp.where(row == lax.div(col, 2), 1.0, 0.0).astype(jnp.bfloat16)
    usable = []
    for j in range(flags_ref.shape[1] // LANES):
        some = flags_ref[:, j * LANES : (j + 1) * LANES].astype(jnp.float32)
        some = jnp.broadcast_to(some, (8, LANES)).astype(jnp.bfloat16)
        usable.append(jnp.dot(some, spread, preferred_element_type=jnp.float32))
    usable = usable[0] if len(usable) == 1 else jnp.concatenate(usable, 1)
    usable = jnp.concatenate([usable] * (rows // 8), 0)
    gr, gi = [], []
    for g in range(groups):
        a, b = gr_ref[g * cg : (g + 1) * cg], gi_ref[g * cg : (g + 1) * cg]
        gr += [a, a]
        gi += [-b, b]
    gr = jnp.concatenate(gr, 0) * usable
    gi = jnp.concatenate(gi, 0) * usable
    low = lax.rem(lax.broadcasted_iota(jnp.int32, (rows, width), 0), 2 * cg) < cg
    for k, ref in ((3, own_ref), (2, one_ref), (1, two_ref), (0, three_ref)):
        s = acc_ref[k * rows : (k + 1) * rows]
        if k in PAIR_TAPS:
            i = TAPS + PAIR_TAPS.index(k)
            s = s + acc_ref[i * rows : (i + 1) * rows]
        other = jnp.where(low, pltpu.roll(s, rows - cg, 0), pltpu.roll(s, cg, 0))
        ref[...] = (gr * s + gi * other).astype(ref.dtype)


def front(samples, channel_index, gain_real, gain_imag, flags, groups):
    _, points, width = samples.shape
    channels = gain_real.shape[0]
    rows = 2 * channels
    depth = (TAPS + len(PAIR_TAPS)) * rows
    flags = flags.reshape(1, -1)
    return pl.pallas_call(
        functools.partial(front_body, groups=groups),
        name="front",
        out_shape=[jax.ShapeDtypeStruct((rows, width), jnp.float32)]
        + [jax.ShapeDtypeStruct((rows, width), jnp.bfloat16)] * 3,
        in_specs=[IN_HBM] * 5,
        out_specs=[IN_VMEM] * 4,
        scratch_shapes=[
            pltpu.SMEM(channel_index.shape, jnp.int32),
            pltpu.VMEM(gain_real.shape, jnp.float32),
            pltpu.VMEM(gain_imag.shape, jnp.float32),
            pltpu.VMEM(flags.shape, jnp.int32),
            pltpu.VMEM((points, width), samples.dtype),
            pltpu.VMEM((TAPS, points // LANES, LANES), jnp.float32),
            pltpu.VMEM((depth, points), jnp.bfloat16),
            pltpu.VMEM((depth, width), jnp.float32),
            pltpu.SemaphoreType.DMA((SPLITS,)),
            pltpu.SemaphoreType.DMA((4,)),
        ],
        compiler_params=pltpu.CompilerParams(vmem_limit_bytes=VMEM_BYTES),
    )(*in_hbm(channel_index, samples, gain_real, gain_imag, flags))


def combine_body(own_ref, one_ref, two_ref, three_ref, *refs):
    out_refs, total_ref = refs[:-1], refs[-1]
    groups, size, _ = total_ref.shape
    total = own_ref[...]
    for ref in (one_ref, two_ref, three_ref):
        total = total + ref[...].astype(jnp.float32)
    for g in range(groups):
        total_ref[g] = total[g * size : (g + 1) * size]
    me = lax.axis_index("chan")
    for j, ref in enumerate(out_refs):
        ref[...] = total_ref[lax.rem(me + j, groups)].astype(jnp.bfloat16)


def combine(own, one, two, three, groups):
    rows, width = own.shape
    piece = jax.ShapeDtypeStruct((rows // groups, width), jnp.bfloat16)
    return pl.pallas_call(
        combine_body,
        name="combine",
        out_shape=[piece] * groups,
        in_specs=[IN_VMEM] * 4,
        out_specs=[IN_VMEM] * groups,
        scratch_shapes=[pltpu.VMEM((groups, rows // groups, width), jnp.float32)],
        compiler_params=pltpu.CompilerParams(vmem_limit_bytes=VMEM_BYTES),
    )(own, one, two, three)


def correlate_body(volts_ref, out_ref, all_ref, left_ref, right_ref, tile_ref, sems, *, tile):
    frames, chunks, size, width = volts_ref.shape
    cg = size // 2
    depth = frames * size
    rows, cols = out_ref.shape[2:]
    me = lax.axis_index("chan")
    piece_of = lambda chunk: lax.rem(me - chunk + chunks, chunks)
    for f in range(frames):
        for j in range(chunks):
            all_ref[j, f * size : (f + 1) * size, :] = volts_ref[f, j].astype(jnp.float32)
    n_row, n_col = rows // width, cols // width
    lane = lax.broadcasted_iota(jnp.int32, (width, depth), 1)
    for q in range(n_row):
        turned = (all_ref[piece_of(lax.axis_index("row") * n_row + q)] * (1.0 / frames)).T
        for c in range(cg):
            mine = jnp.where(lax.rem(lane, cg) == c, turned, 0.0)
            left_ref[c, q * width : (q + 1) * width, :] = mine.astype(jnp.bfloat16)
    low = lax.rem(lax.broadcasted_iota(jnp.int32, (depth, width), 0), size) < cg
    for q in range(n_col):
        x = all_ref[piece_of(lax.axis_index("tm") * n_col + q)]
        part = slice(q * width, (q + 1) * width)
        right_ref[0, :, part] = x.astype(jnp.bfloat16)
        crossed = jnp.where(low, -pltpu.roll(x, depth - cg, 0), pltpu.roll(x, cg, 0))
        right_ref[1, :, part] = crossed.astype(jnp.bfloat16)

    high, wide = min(tile, rows), min(tile, cols)
    spots = [(top, left) for left in range(0, cols, wide) for top in range(0, rows, high)]
    total = 2 * cg

    def copy(n, s):
        top, left = spots[s]
        slot = lax.rem(n, 2)
        return pltpu.make_async_copy(
            tile_ref.at[slot, pl.ds(top, high), pl.ds(left, wide)],
            out_ref.at[lax.rem(n, 2), lax.div(n, 2), pl.ds(top, high), pl.ds(left, wide)],
            sems.at[slot, s],
        )

    def step(n, carry):
        @pl.when(n >= 2)
        def _():
            for s in range(len(spots)):
                copy(n - 2, s).wait()

        for s, (top, left) in enumerate(spots):
            product = jnp.dot(
                left_ref[lax.div(n, 2), top : top + high, :],
                right_ref[lax.rem(n, 2), :, left : left + wide],
                preferred_element_type=jnp.float32,
            )
            tile_ref[lax.rem(n, 2), top : top + high, left : left + wide] = product.astype(jnp.bfloat16)
            copy(n, s).start()
        return carry

    lax.fori_loop(0, total, step, 0)
    for n in range(total - 2, total):
        for s in range(len(spots)):
            copy(n, s).wait()


def correlate(volts, rows, cols):
    frames, chunks, size, width = volts.shape
    cg = size // 2
    depth = frames * size
    spots = (rows // min(TILE, rows)) * (cols // min(TILE, cols))
    return pl.pallas_call(
        functools.partial(correlate_body, tile=TILE),
        name="correlate",
        out_shape=jax.ShapeDtypeStruct((2, cg, rows, cols), jnp.bfloat16),
        in_specs=[IN_VMEM],
        out_specs=IN_HBM,
        scratch_shapes=[
            pltpu.VMEM((chunks, depth, width), jnp.float32),
            pltpu.VMEM((cg, rows, depth), jnp.bfloat16),
            pltpu.VMEM((2, depth, cols), jnp.bfloat16),
            pltpu.VMEM((2, rows, cols), jnp.bfloat16),
            pltpu.SemaphoreType.DMA((2, spots)),
        ],
        compiler_params=pltpu.CompilerParams(vmem_limit_bytes=VMEM_BYTES),
    )(volts)


def local(samples, channel_index, gain_real, gain_imag, flags):
    planes = lax.axis_size("chan")
    inputs_total = samples.shape[2] * planes
    own, one, two, three = front(samples, channel_index, gain_real, gain_imag, flags, planes)
    one = shifted(one, FRAME_AXES, 1, False)
    two = shifted(two, FRAME_AXES, 2, False)
    three = shifted(three, FRAME_AXES, 3, False)
    pieces = combine(own, one, two, three, planes)
    pieces = [piece if j == 0 else shifted(piece, "chan", j, True) for j, piece in enumerate(pieces)]
    volts = lax.all_gather(jnp.stack(pieces), FRAME_AXES, axis=0)
    return correlate(volts, inputs_total // lax.axis_size("row"), inputs_total // lax.axis_size("tm"))


def solution(mesh):
    in_specs = (P(("tm", "row"), None, "chan"), P(), P(None, "chan"), P(None, "chan"), P("chan"))
    out_specs = P(None, "chan", "row", "tm")
    return jax.shard_map(local, mesh=mesh, in_specs=in_specs, out_specs=out_specs, check_vma=False)
```

time: 150 us -> 46.3 us (0.31)
  local copies, waits for them, and re-layouts: 43.7 us -> 0 us
  other arithmetic: 36.9 us -> 0.01 us
  matrix products: 29.2 us -> 0 us
  Pallas kernels: 0 us -> 15.9 us
  blocking collectives: 16 us -> 9.23 us
  waiting for transfers between devices: 7.24 us -> 4.26 us
    another operation x2 -> x0, local copies, waits for them, and re-layouts: 42.7 us -> none  [the longest x1 42 us: local(): jnp.stack([product[:, :, :col_count], product[:, :, col_count:]], 0)]
    convert_element_type x2 -> x0, other arithmetic: 33.4 us -> none  [the longest x1 32.7 us: local(): return result.astype(jnp.bfloat16)]
    dot_general x2 -> x0, matrix products: 29.2 us -> none  [the longest x1 23.1 us: local(): jnp.einsum('fcr,fcq->crq', left_side, right_side, preferred_element_type=...]
    pallas_call x0 -> x3, Pallas kernels: none -> 15.9 us  [the longest x1 11.7 us: correlate(): pl.pallas_call(functools.partial(correlate_body, tile=TILE), name='correl...]
    all_gather x2 -> x1, blocking collectives: 16 us -> 9.23 us  [local(): volts = lax.all_gather(jnp.stack(pieces), FRAME_AXES, axis=0)]
    all_to_all x1 -> x0, waiting for transfers between devices: 5.74 us -> none  [local(): lax.all_to_all(turned, 'chan', split_axis=2, concat_axis=3, tiled=True)]
    ppermute x3 -> x6, starting transfers between devices: 11.4 us -> 16.7 us  [shifted(): return lax.ppermute(value, axis, pairs)]
    all_to_all x1 -> x0, starting transfers between devices: 4.87 us -> none  [local(): lax.all_to_all(turned, 'chan', split_axis=2, concat_axis=3, tiled=True)]
  transfers between devices with their start and end apart: 4 -> 6, of which waited for: 2 -> 3; matrix products, arithmetic and copies ran while one was open for 1% -> 0% of each run, Pallas kernels for 0% -> 0%
where the time goes in v1:
time: 46.3 us; the launch traced here: 46.1 us
  starting transfers between devices  16.7 us (36%)
  Pallas kernels  15.9 us (34%)
  blocking collectives  9.23 us (20%)
  waiting for transfers between devices  4.26 us (9%)
    ppermute x6, starting transfers between devices, shifted(): return lax.ppermute(value, axis, pairs)  16.7 us
    pallas_call x1, Pallas kernels, correlate(): pl.pallas_call(functools.partial(correlate_body, tile=TILE), name='correl...  11.7 us
    all_gather x1, blocking collectives, local(): volts = lax.all_gather(jnp.stack(pieces), FRAME_AXES, axis=0)  9.23 us
    ppermute x6, waiting for transfers between devices, shifted(): return lax.ppermute(value, axis, pairs)  4.26 us
    pallas_call x1, Pallas kernels, front(): pl.pallas_call(functools.partial(front_body, groups=groups), name='front'...  4.15 us
  transfers between devices with their start and end apart: 6, of which 3 were waited for; matrix products, arithmetic and copies ran while one was open for 0% of the time, Pallas kernels for 0%

profile of v1, /device:TPU:0, one launch (start us, length us, event | category | flops | bytes accessed | tf_op | source)
XLA Modules:
  0.0 46.1 jit_solution(17373516729689710174)
XLA Ops:
  0.0 4.2 %front.1 = (f32[32,1024]{1,0:T(8,128)S(1)}, bf16[32,1024]{1,0:T(8,128)(2,1)S(1)}, bf16[32,1024]{1,0:T(8,128)(2,1)S(1)}, bf16[32,1024]{1,0:T(8,128)(2,1)S(1)}) custom-call(s32[16]{0:T(128)} %index_hbm.1, bf16[1,4096,1024]{2,1,0:T(8,128)(2,1)} %samples_ref.1, f32[16,1024]{1,0:T(8,128)} %gr_hbm.1, f32[16,1024]{1,0:T(8,128)} %gi_hbm.1, s32[1,512]{1,0:T(1,128)} %bitcast.11), custom_call_target="tpu_custom_call" | custom-call | tf_op jit(solution)/shard_map/front/pallas_call | solution.py:155
  4.2 2.4 %collective-permute-start = (bf16[32,1024]{1,0:T(8,128)(2,1)S(1)}, bf16[32,1024]{1,0:T(8,128)(2,1)S(1)}, u32[]{:S(2)}, u32[]{:S(2)}) collective-permute-start(bf16[32,1024]{1,0:T(8,128)(2,1)S(1)} %get-tuple-element.14), channel_id=1, source_target_pairs={{0,1},{1,2},{2,3},{3,4},{4,5},{5,6},{6,7},{8,9},{9,10},{10,11},{11... | collective-permute-start | bytes 196616 | tf_op jit(solution)/shard_map/ppermute | solution.py:30
  6.6 4.4 %collective-permute-start.1 = (bf16[32,1024]{1,0:T(8,128)(2,1)S(1)}, bf16[32,1024]{1,0:T(8,128)(2,1)S(1)}, u32[]{:S(2)}, u32[]{:S(2)}) collective-permute-start(bf16[32,1024]{1,0:T(8,128)(2,1)S(1)} %get-tuple-element.15), channel_id=1, source_target_pairs={{0,2},{1,3},{2,4},{3,5},{4,6},{5,7},{8,10},{9,11},{10,12},{11,13},... | collective-permute-start | bytes 196616 | tf_op jit(solution)/shard_map/ppermute | solution.py:30
  11.0 4.3 %collective-permute-start.2 = (bf16[32,1024]{1,0:T(8,128)(2,1)S(1)}, bf16[32,1024]{1,0:T(8,128)(2,1)S(1)}, u32[]{:S(2)}, u32[]{:S(2)}) collective-permute-start(bf16[32,1024]{1,0:T(8,128)(2,1)S(1)} %get-tuple-element.16), channel_id=1, source_target_pairs={{0,3},{1,4},{2,5},{3,6},{4,7},{8,11},{9,12},{10,13},{11,14},{12,15... | collective-permute-start | bytes 196616 | tf_op jit(solution)/shard_map/ppermute | solution.py:30
  15.3 0.0 collective-permute-done.one_ref
  15.3 0.0 collective-permute-done.1.two_ref
  15.3 1.9 %collective-permute-done.2.three_ref = bf16[32,1024]{1,0:T(8,128)(2,1)S(1)} collective-permute-done((bf16[32,1024]{1,0:T(8,128)(2,1)S(1)}, bf16[32,1024]{1,0:T(8,128)(2,1)S(1)}, u32[]{:S(2)}, u32[]{:S(2)}) %collective-permute-start.2) | collective-permute-done | bytes 65568 | tf_op jit(solution)/shard_map/ppermute | solution.py:30
  17.2 1.6 %collective-permute-start.3 = (bf16[8,1024]{1,0:T(8,128)(2,1)S(1)}, bf16[8,1024]{1,0:T(8,128)(2,1)S(1)}, u32[]{:S(2)}, u32[]{:S(2)}) collective-permute-start(bf16[8,1024]{1,0:T(8,128)(2,1)S(1)} %get-tuple-element.18), channel_id=1, source_target_pairs={{0,8},{8,16},{16,24},{24,0},{1,9},{9,17},{17,25},{25,1},{2,10},{10... | collective-permute-start | bytes 49160 | tf_op jit(solution)/shard_map/ppermute | solution.py:30
  18.9 2.6 %collective-permute-start.4 = (bf16[8,1024]{1,0:T(8,128)(2,1)S(1)}, bf16[8,1024]{1,0:T(8,128)(2,1)S(1)}, u32[]{:S(2)}, u32[]{:S(2)}) collective-permute-start(bf16[8,1024]{1,0:T(8,128)(2,1)S(1)} %get-tuple-element.19), channel_id=1, source_target_pairs={{0,16},{8,24},{16,0},{24,8},{1,17},{9,25},{17,1},{25,9},{2,18},{10... | collective-permute-start | bytes 49160 | tf_op jit(solution)/shard_map/ppermute | solution.py:30
  21.4 1.3 %collective-permute-start.5 = (bf16[8,1024]{1,0:T(8,128)(2,1)S(1)}, bf16[8,1024]{1,0:T(8,128)(2,1)S(1)}, u32[]{:S(2)}, u32[]{:S(2)}) collective-permute-start(bf16[8,1024]{1,0:T(8,128)(2,1)S(1)} %get-tuple-element.20), channel_id=1, source_target_pairs={{0,24},{8,0},{16,8},{24,16},{1,25},{9,1},{17,9},{25,17},{2,26},{10... | collective-permute-start | bytes 49160 | tf_op jit(solution)/shard_map/ppermute | solution.py:30
  22.8 0.0 collective-permute-done.3
  22.8 0.7 %collective-permute-done.4 = bf16[8,1024]{1,0:T(8,128)(2,1)S(1)} collective-permute-done((bf16[8,1024]{1,0:T(8,128)(2,1)S(1)}, bf16[8,1024]{1,0:T(8,128)(2,1)S(1)}, u32[]{:S(2)}, u32[]{:S(2)}) %collective-permute-start.4) | collective-permute-done | bytes 16416 | tf_op jit(solution)/shard_map/ppermute | solution.py:30
  23.5 1.7 %collective-permute-done.5 = bf16[8,1024]{1,0:T(8,128)(2,1)S(1)} collective-permute-done((bf16[8,1024]{1,0:T(8,128)(2,1)S(1)}, bf16[8,1024]{1,0:T(8,128)(2,1)S(1)}, u32[]{:S(2)}, u32[]{:S(2)}) %collective-permute-start.5) | collective-permute-done | bytes 16416 | tf_op jit(solution)/shard_map/ppermute | solution.py:30
  25.2 9.2 %all-gather = bf16[32,8,1024]{2,1,0:T(8,128)(2,1)S(1)} all-gather(bf16[4,8,1024]{2,1,0:T(8,128)(2,1)S(1)} %pad_maximum_fusion), channel_id=2, replica_groups=mesh['chan'=4,'tm'=2,'row'=4] {'tm','row'}, dimensions={0}, use_global_device_ids=true | all-gather | bytes 589824 | tf_op jit(solution)/shard_map/all_gather | solution.py:296
  34.4 11.7 %correlate.1 = bf16[2,4,1024,2048]{3,2,1,0:T(8,128)(2,1)} custom-call(bf16[8,4,8,1024]{3,2,1,0:T(8,128)(2,1)S(1)} %bitcast.6), custom_call_target="tpu_custom_call" | custom-call | tf_op jit(solution)/shard_map/correlate/pallas_call | solution.py:270
  (2 shorter events, 0.1 us)
Async XLA Ops:
  4.2 11.1 %collective-permute-start = (bf16[32,1024]{1,0:T(8,128)(2,1)S(1)}, bf16[32,1024]{1,0:T(8,128)(2,1)S(1)}, u32[]{:S(2)}, u32[]{:S(2)}) collective-permute-start(bf16[32,1024]{1,0:T(8,128)(2,1)S(1)} %get-tuple-element.14), channel_id=1, source_target_pairs={{0,1},{1,2},{2,3},{3,4},{4,5},{5,6},{6,7},{8,9},{9,10},{10,11},{11... | collective-permute-start | bytes 196616 | tf_op jit(solution)/shard_map/ppermute | solution.py:30
  6.6 8.7 %collective-permute-start.1 = (bf16[32,1024]{1,0:T(8,128)(2,1)S(1)}, bf16[32,1024]{1,0:T(8,128)(2,1)S(1)}, u32[]{:S(2)}, u32[]{:S(2)}) collective-permute-start(bf16[32,1024]{1,0:T(8,128)(2,1)S(1)} %get-tuple-element.15), channel_id=1, source_target_pairs={{0,2},{1,3},{2,4},{3,5},{4,6},{5,7},{8,10},{9,11},{10,12},{11,13},... | collective-permute-start | bytes 196616 | tf_op jit(solution)/shard_map/ppermute | solution.py:30
  11.0 6.2 %collective-permute-start.2 = (bf16[32,1024]{1,0:T(8,128)(2,1)S(1)}, bf16[32,1024]{1,0:T(8,128)(2,1)S(1)}, u32[]{:S(2)}, u32[]{:S(2)}) collective-permute-start(bf16[32,1024]{1,0:T(8,128)(2,1)S(1)} %get-tuple-element.16), channel_id=1, source_target_pairs={{0,3},{1,4},{2,5},{3,6},{4,7},{8,11},{9,12},{10,13},{11,14},{12,15... | collective-permute-start | bytes 196616 | tf_op jit(solution)/shard_map/ppermute | solution.py:30
  17.2 5.6 %collective-permute-start.3 = (bf16[8,1024]{1,0:T(8,128)(2,1)S(1)}, bf16[8,1024]{1,0:T(8,128)(2,1)S(1)}, u32[]{:S(2)}, u32[]{:S(2)}) collective-permute-start(bf16[8,1024]{1,0:T(8,128)(2,1)S(1)} %get-tuple-element.18), channel_id=1, source_target_pairs={{0,8},{8,16},{16,24},{24,0},{1,9},{9,17},{17,25},{25,1},{2,10},{10... | collective-permute-start | bytes 49160 | tf_op jit(solution)/shard_map/ppermute | solution.py:30
  18.9 4.6 %collective-permute-start.4 = (bf16[8,1024]{1,0:T(8,128)(2,1)S(1)}, bf16[8,1024]{1,0:T(8,128)(2,1)S(1)}, u32[]{:S(2)}, u32[]{:S(2)}) collective-permute-start(bf16[8,1024]{1,0:T(8,128)(2,1)S(1)} %get-tuple-element.19), channel_id=1, source_target_pairs={{0,16},{8,24},{16,0},{24,8},{1,17},{9,25},{17,1},{25,9},{2,18},{10... | collective-permute-start | bytes 49160 | tf_op jit(solution)/shard_map/ppermute | solution.py:30
  21.4 3.7 %collective-permute-start.5 = (bf16[8,1024]{1,0:T(8,128)(2,1)S(1)}, bf16[8,1024]{1,0:T(8,128)(2,1)S(1)}, u32[]{:S(2)}, u32[]{:S(2)}) collective-permute-start(bf16[8,1024]{1,0:T(8,128)(2,1)S(1)} %get-tuple-element.20), channel_id=1, source_target_pairs={{0,24},{8,0},{16,8},{24,16},{1,25},{9,1},{17,9},{25,17},{2,26},{10... | collective-permute-start | bytes 49160 | tf_op jit(solution)/shard_map/ppermute | solution.py:30

commit v2 on v1

--- a/solution.py
+++ b/solution.py
@@ -24,10 +24,9 @@
     return [pltpu.with_memory_space_constraint(a, pltpu.HBM) for a in arrays]
 
 
-def shifted(value, axis, by, wrap):
+def rotated(value, axis, by):
     peers = lax.axis_size(axis)
-    pairs = [(i, (i + by) % peers) for i in range(peers) if wrap or i + by < peers]
-    return lax.ppermute(value, axis, pairs)
+    return lax.ppermute(value, axis, [(i, (i + by) % peers) for i in range(peers)])
 
 
 def sine_quarter(x):
@@ -52,7 +51,7 @@
 
 def front_body(
     index_hbm, samples_ref, gr_hbm, gi_hbm, flags_hbm,
-    own_ref, one_ref, two_ref, three_ref,
+    keep_ref, give_ref,
     index_ref, gr_ref, gi_ref, flags_ref, block_ref, filter_ref, table_ref, acc_ref, sems, small_sems,
     *, groups,
 ):
@@ -137,13 +136,18 @@
     gr = jnp.concatenate(gr, 0) * usable
     gi = jnp.concatenate(gi, 0) * usable
     low = lax.rem(lax.broadcasted_iota(jnp.int32, (rows, width), 0), 2 * cg) < cg
-    for k, ref in ((3, own_ref), (2, one_ref), (1, two_ref), (0, three_ref)):
+    core = lax.rem(lax.axis_index("row"), 2)
+    half = rows // 2
+    for k in range(TAPS):
         s = acc_ref[k * rows : (k + 1) * rows]
         if k in PAIR_TAPS:
             i = TAPS + PAIR_TAPS.index(k)
             s = s + acc_ref[i * rows : (i + 1) * rows]
         other = jnp.where(low, pltpu.roll(s, rows - cg, 0), pltpu.roll(s, cg, 0))
-        ref[...] = (gr * s + gi * other).astype(ref.dtype)
+        volts = gr * s + gi * other
+        first, second = volts[:half], volts[half:]
+        keep_ref[k] = jnp.where(core == 0, first, second)
+        give_ref[k] = jnp.where(core == 0, second, first).astype(give_ref.dtype)
 
 
 def front(samples, channel_index, gain_real, gain_imag, flags, groups):
@@ -155,10 +159,12 @@
     return pl.pallas_call(
         functools.partial(front_body, groups=groups),
         name="front",
-        out_shape=[jax.ShapeDtypeStruct((rows, width), jnp.float32)]
-        + [jax.ShapeDtypeStruct((rows, width), jnp.bfloat16)] * 3,
+        out_shape=[
+            jax.ShapeDtypeStruct((TAPS, rows // 2, width), jnp.float32),
+            jax.ShapeDtypeStruct((TAPS, rows // 2, width), jnp.bfloat16),
+        ],
         in_specs=[IN_HBM] * 5,
-        out_specs=[IN_VMEM] * 4,
+        out_specs=[IN_VMEM] * 2,
         scratch_shapes=[
             pltpu.SMEM(channel_index.shape, jnp.int32),
             pltpu.VMEM(gain_real.shape, jnp.float32),
@@ -175,53 +181,92 @@
     )(*in_hbm(channel_index, samples, gain_real, gain_imag, flags))
 
 
-def combine_body(own_ref, one_ref, two_ref, three_ref, *refs):
+def pair_body(keep_ref, got_ref, here_ref, next_ref, after_ref):
+    even = lax.rem(lax.axis_index("row"), 2) == 0
+    half = keep_ref.shape[1]
+    first, second = [], []
+    for k in range(TAPS):
+        keep, got = keep_ref[k], got_ref[k].astype(jnp.float32)
+        first.append(jnp.where(even, keep, got))
+        second.append(jnp.where(even, got, keep))
+    here_ref[0] = first[3]
+    here_ref[1] = first[2] + second[3]
+    next_ref[:half] = (first[1] + second[2]).astype(next_ref.dtype)
+    next_ref[half:] = (first[0] + second[1]).astype(next_ref.dtype)
+    after_ref[...] = second[0].astype(after_ref.dtype)
+
+
+def pair_sum(keep, got):
+    _, half, width = keep.shape
+    return pl.pallas_call(
+        pair_body,
+        name="pair_sum",
+        out_shape=[
+            jax.ShapeDtypeStruct((2, half, width), jnp.float32),
+            jax.ShapeDtypeStruct((2 * half, width), jnp.bfloat16),
+            jax.ShapeDtypeStruct((half, width), jnp.bfloat16),
+        ],
+        in_specs=[IN_VMEM] * 2,
+        out_specs=[IN_VMEM] * 3,
+        compiler_params=pltpu.CompilerParams(vmem_limit_bytes=VMEM_BYTES),
+    )(keep, got)
+
+
+def combine_body(here_ref, next_ref, after_ref, *refs):
     out_refs, total_ref = refs[:-1], refs[-1]
     groups, size, _ = total_ref.shape
-    total = own_ref[...]
-    for ref in (one_ref, two_ref, three_ref):
-        total = total + ref[...].astype(jnp.float32)
+    size = size // 2
+    half = after_ref.shape[0]
+    chip = lax.axis_index("tm") * (lax.axis_size("row") // 2) + lax.div(lax.axis_index("row"), 2)
+    even = here_ref[0] + jnp.where(chip >= 1, next_ref[:half].astype(jnp.float32), 0.0)
+    even = even + jnp.where(chip >= 2, after_ref[...].astype(jnp.float32), 0.0)
+    odd = here_ref[1] + jnp.where(chip >= 1, next_ref[half:].astype(jnp.float32), 0.0)
     for g in range(groups):
-        total_ref[g] = total[g * size : (g + 1) * size]
+        total_ref[g, :size] = even[g * size : (g + 1) * size]
+        total_ref[g, size:] = odd[g * size : (g + 1) * size]
     me = lax.axis_index("chan")
     for j, ref in enumerate(out_refs):
         ref[...] = total_ref[lax.rem(me + j, groups)].astype(jnp.bfloat16)
 
 
-def combine(own, one, two, three, groups):
-    rows, width = own.shape
-    piece = jax.ShapeDtypeStruct((rows // groups, width), jnp.bfloat16)
+def combine(here, following, after, groups):
+    half, width = after.shape
+    size = 2 * (half // groups)
+    piece = jax.ShapeDtypeStruct((size, width), jnp.bfloat16)
     return pl.pallas_call(
         combine_body,
         name="combine",
         out_shape=[piece] * groups,
-        in_specs=[IN_VMEM] * 4,
+        in_specs=[IN_VMEM] * 3,
         out_specs=[IN_VMEM] * groups,
-        scratch_shapes=[pltpu.VMEM((groups, rows // groups, width), jnp.float32)],
+        scratch_shapes=[pltpu.VMEM((groups, size, width), jnp.float32)],
         compiler_params=pltpu.CompilerParams(vmem_limit_bytes=VMEM_BYTES),
-    )(own, one, two, three)
-
-
-def correlate_body(volts_ref, out_ref, all_ref, left_ref, right_ref, tile_ref, sems, *, tile):
-    frames, chunks, size, width = volts_ref.shape
+    )(here, following, after)
+
+
+def correlate_body(mine_ref, other_ref, out_ref, all_ref, left_ref, right_ref, tile_ref, sems, *, tile):
+    chips, chunks, size, width = mine_ref.shape
+    depth = chips * size
+    size = size // 2
     cg = size // 2
-    depth = frames * size
+    frames = 2 * chips
     rows, cols = out_ref.shape[2:]
-    me = lax.axis_index("chan")
-    piece_of = lambda chunk: lax.rem(me - chunk + chunks, chunks)
-    for f in range(frames):
+    core = lax.rem(lax.axis_index("row"), 2)
+    for ref, half in ((mine_ref, core), (other_ref, 1 - core)):
         for j in range(chunks):
-            all_ref[j, f * size : (f + 1) * size, :] = volts_ref[f, j].astype(jnp.float32)
+            chunk = half * chunks + lax.rem(lax.axis_index("chan") + chunks - j, chunks)
+            for m in range(chips):
+                all_ref[chunk, m * 2 * size : (m + 1) * 2 * size, :] = ref[m, j].astype(jnp.float32)
     n_row, n_col = rows // width, cols // width
     lane = lax.broadcasted_iota(jnp.int32, (width, depth), 1)
     for q in range(n_row):
-        turned = (all_ref[piece_of(lax.axis_index("row") * n_row + q)] * (1.0 / frames)).T
+        turned = (all_ref[lax.axis_index("row") * n_row + q] * (1.0 / frames)).T
         for c in range(cg):
             mine = jnp.where(lax.rem(lane, cg) == c, turned, 0.0)
             left_ref[c, q * width : (q + 1) * width, :] = mine.astype(jnp.bfloat16)
     low = lax.rem(lax.broadcasted_iota(jnp.int32, (depth, width), 0), size) < cg
     for q in range(n_col):
-        x = all_ref[piece_of(lax.axis_index("tm") * n_col + q)]
+        x = all_ref[lax.axis_index("tm") * n_col + q]
         part = slice(q * width, (q + 1) * width)
         right_ref[0, :, part] = x.astype(jnp.bfloat16)
         crossed = jnp.where(low, -pltpu.roll(x, depth - cg, 0), pltpu.roll(x, cg, 0))
@@ -262,39 +307,56 @@
             copy(n, s).wait()
 
 
-def correlate(volts, rows, cols):
-    frames, chunks, size, width = volts.shape
-    cg = size // 2
-    depth = frames * size
+def correlate(mine, other, rows, cols):
+    chips, chunks, size, width = mine.shape
+    cg = size // 4
+    depth = chips * size
     spots = (rows // min(TILE, rows)) * (cols // min(TILE, cols))
     return pl.pallas_call(
         functools.partial(correlate_body, tile=TILE),
         name="correlate",
         out_shape=jax.ShapeDtypeStruct((2, cg, rows, cols), jnp.bfloat16),
-        in_specs=[IN_VMEM],
+        in_specs=[IN_VMEM] * 2,
         out_specs=IN_HBM,
         scratch_shapes=[
-            pltpu.VMEM((chunks, depth, width), jnp.float32),
+            pltpu.VMEM((2 * chunks, depth, width), jnp.float32),
             pltpu.VMEM((cg, rows, depth), jnp.bfloat16),
             pltpu.VMEM((2, depth, cols), jnp.bfloat16),
             pltpu.VMEM((2, rows, cols), jnp.bfloat16),
             pltpu.SemaphoreType.DMA((2, spots)),
         ],
         compiler_params=pltpu.CompilerParams(vmem_limit_bytes=VMEM_BYTES),
-    )(volts)
+    )(mine, other)
+
+
+def turn_plane(value, by):
+    planes, rows = lax.axis_size("chan"), lax.axis_size("row")
+    half = planes // 2
+    pairs = []
+    for c in range(planes):
+        for r in range(rows):
+            to = (r % 2) * half + (c + by) % half
+            pairs.append((c * rows + r, to * rows + r - r % 2 + c // half))
+    return lax.ppermute(value, ("chan", "row"), pairs)
+
+
+def swapped(value):
+    peers = lax.axis_size(FRAME_AXES)
+    return lax.ppermute(value, FRAME_AXES, [(i, i ^ 1) for i in range(peers)])
 
 
 def local(samples, channel_index, gain_real, gain_imag, flags):
     planes = lax.axis_size("chan")
+    chips = lax.axis_size(FRAME_AXES) // 2
     inputs_total = samples.shape[2] * planes
-    own, one, two, three = front(samples, channel_index, gain_real, gain_imag, flags, planes)
-    one = shifted(one, FRAME_AXES, 1, False)
-    two = shifted(two, FRAME_AXES, 2, False)
-    three = shifted(three, FRAME_AXES, 3, False)
-    pieces = combine(own, one, two, three, planes)
-    pieces = [piece if j == 0 else shifted(piece, "chan", j, True) for j, piece in enumerate(pieces)]
-    volts = lax.all_gather(jnp.stack(pieces), FRAME_AXES, axis=0)
-    return correlate(volts, inputs_total // lax.axis_size("row"), inputs_total // lax.axis_size("tm"))
+    keep, give = front(samples, channel_index, gain_real, gain_imag, flags, planes)
+    here, following, after = pair_sum(keep, swapped(give))
+    following = rotated(following, FRAME_AXES, 2)
+    after = rotated(after, FRAME_AXES, 4)
+    pieces = combine(here, following, after, planes // 2)
+    pieces = jnp.stack([turn_plane(piece, j) for j, piece in enumerate(pieces)])
+    mine = jnp.stack([pieces] + [rotated(pieces, FRAME_AXES, 2 * s) for s in range(1, chips)])
+    return correlate(mine, swapped(mine), inputs_total // lax.axis_size("row"), inputs_total // lax.axis_size("tm"))
 
 
 def solution(mesh):

time: 46.3 us -> 41.2 us (0.89)
  blocking collectives: 9.23 us -> 0 us
  waiting for transfers between devices: 4.26 us -> 9.08 us
  starting transfers between devices: 16.7 us -> 16 us
    all_gather x1 -> x0, blocking collectives: 9.23 us -> none  [local(): volts = lax.all_gather(jnp.stack(pieces), FRAME_AXES, axis=0)]
    ppermute x6 -> x9, waiting for transfers between devices: 4.26 us -> 9.08 us  [the longest x5 4.79 us: rotated(): lax.ppermute(value, axis, [(i, (i + by) % peers) for i in range(peers)])]
    ppermute x6 -> x9, starting transfers between devices: 16.7 us -> 16 us  [the longest x5 9.1 us: rotated(): lax.ppermute(value, axis, [(i, (i + by) % peers) for i in range(peers)])]
  transfers between devices with their start and end apart: 6 -> 9, of which waited for: 3 -> 5; matrix products, arithmetic and copies ran while one was open for 0% -> 0% of each run, Pallas kernels for 0% -> 0%
where the time goes in v2:
time: 41.2 us; the launch traced here: 41.1 us
  starting transfers between devices  16 us (39%)
  Pallas kernels  15.9 us (39%)
  waiting for transfers between devices  9.08 us (22%)
    pallas_call x1, Pallas kernels, correlate(): pl.pallas_call(functools.partial(correlate_body, tile=TILE), name='correl...  11.7 us
    ppermute x5, starting transfers between devices, rotated(): lax.ppermute(value, axis, [(i, (i + by) % peers) for i in range(peers)])  9.1 us
    ppermute x5, waiting for transfers between devices, rotated(): lax.ppermute(value, axis, [(i, (i + by) % peers) for i in range(peers)])  4.79 us
    ppermute x2, starting transfers between devices, swapped(): return lax.ppermute(value, FRAME_AXES, [(i, i ^ 1) for i in range(peers)])  4.37 us
    pallas_call x1, Pallas kernels, front(): pl.pallas_call(functools.partial(front_body, groups=groups), name='front'...  4.17 us
    ppermute x2, starting transfers between devices, turn_plane(): return lax.ppermute(value, ('chan', 'row'), pairs)  2.5 us
    ppermute x2, waiting for transfers between devices, swapped(): return lax.ppermute(value, FRAME_AXES, [(i, i ^ 1) for i in range(peers)])  2.15 us
    ppermute x2, waiting for transfers between devices, turn_plane(): return lax.ppermute(value, ('chan', 'row'), pairs)  2.14 us
  transfers between devices with their start and end apart: 9, of which 5 were waited for; matrix products, arithmetic and copies ran while one was open for 0% of the time, Pallas kernels for 0%

profile of v2, /device:TPU:0, one launch (start us, length us, event | category | flops | bytes accessed | tf_op | source)
XLA Modules:
  0.0 41.1 jit_solution(8560258216176825006)
XLA Ops:
  0.0 4.2 %front.1 = (f32[4,16,1024]{2,1,0:T(8,128)S(1)}, bf16[4,16,1024]{2,1,0:T(8,128)(2,1)S(1)}) custom-call(s32[16]{0:T(128)} %index_hbm.1, bf16[1,4096,1024]{2,1,0:T(8,128)(2,1)} %samples_ref.1, f32[16,1024]{1,0:T(8,128)} %gr_hbm.1, f32[16,1024]{1,0:T(8,128)} %gi_hbm.1, s32[1,512]{1,0:T(1,128)} %bitcast.13), custom_call_target="tpu_custom_call" | custom-call | tf_op jit(solution)/shard_map/front/pallas_call | solution.py:159
  4.2 0.6 %collective-permute-start = (bf16[4,16,1024]{2,1,0:T(8,128)(2,1)S(1)}, bf16[4,16,1024]{2,1,0:T(8,128)(2,1)S(1)}, u32[]{:S(2)}, u32[]{:S(2)}) collective-permute-start(bf16[4,16,1024]{2,1,0:T(8,128)(2,1)S(1)} %get-tuple-element.13), channel_id=1, source_target_pairs={{0,1},{1,0},{2,3},{3,2},{4,5},{5,4},{6,7},{7,6},{8,9},{9,8},{10,11... | collective-permute-start | bytes 393224 | tf_op jit(solution)/shard_map/ppermute | solution.py:345
  4.7 1.0 %collective-permute-done.got_ref = bf16[4,16,1024]{2,1,0:T(8,128)(2,1)S(1)} collective-permute-done((bf16[4,16,1024]{2,1,0:T(8,128)(2,1)S(1)}, bf16[4,16,1024]{2,1,0:T(8,128)(2,1)S(1)}, u32[]{:S(2)}, u32[]{:S(2)}) %collective-permute-start) | collective-permute-done | bytes 131104 | tf_op jit(solution)/shard_map/ppermute | solution.py:345
  5.8 2.9 %collective-permute-start.1 = (bf16[32,1024]{1,0:T(8,128)(2,1)S(1)}, bf16[32,1024]{1,0:T(8,128)(2,1)S(1)}, u32[]{:S(2)}, u32[]{:S(2)}) collective-permute-start(bf16[32,1024]{1,0:T(8,128)(2,1)S(1)} %get-tuple-element.15), channel_id=1, source_target_pairs={{0,2},{1,3},{2,4},{3,5},{4,6},{5,7},{6,0},{7,1},{8,10},{9,11},{10,... | collective-permute-start | bytes 196616 | tf_op jit(solution)/shard_map/ppermute | solution.py:29
  8.7 1.5 %collective-permute-start.2 = (bf16[16,1024]{1,0:T(8,128)(2,1)S(1)}, bf16[16,1024]{1,0:T(8,128)(2,1)S(1)}, u32[]{:S(2)}, u32[]{:S(2)}) collective-permute-start(bf16[16,1024]{1,0:T(8,128)(2,1)S(1)} %get-tuple-element.16), channel_id=1, source_target_pairs={{0,4},{1,5},{2,6},{3,7},{4,0},{5,1},{6,2},{7,3},{8,12},{9,13},{10,... | collective-permute-start | bytes 98312 | tf_op jit(solution)/shard_map/ppermute | solution.py:29
  10.2 2.5 %collective-permute-done.2.after_ref = bf16[16,1024]{1,0:T(8,128)(2,1)S(1)} collective-permute-done((bf16[16,1024]{1,0:T(8,128)(2,1)S(1)}, bf16[16,1024]{1,0:T(8,128)(2,1)S(1)}, u32[]{:S(2)}, u32[]{:S(2)}) %collective-permute-start.2) | collective-permute-done | bytes 32800 | tf_op jit(solution)/shard_map/ppermute | solution.py:29
  12.7 0.0 collective-permute-done.1.next_ref
  12.8 0.7 %collective-permute-start.3 = (bf16[16,1024]{1,0:T(8,128)(2,1)S(1)}, bf16[16,1024]{1,0:T(8,128)(2,1)S(1)}, u32[]{:S(2)}, u32[]{:S(2)}) collective-permute-start(bf16[16,1024]{1,0:T(8,128)(2,1)S(1)} %get-tuple-element.17), channel_id=1, source_target_pairs={{0,0},{1,16},{2,2},{3,18},{8,8},{9,24},{10,10},{11,26},{16,1},{17,... | collective-permute-start | bytes 98312 | tf_op jit(solution)/shard_map/ppermute | solution.py:340
  13.5 1.8 %collective-permute-start.4 = (bf16[16,1024]{1,0:T(8,128)(2,1)S(1)}, bf16[16,1024]{1,0:T(8,128)(2,1)S(1)}, u32[]{:S(2)}, u32[]{:S(2)}) collective-permute-start(bf16[16,1024]{1,0:T(8,128)(2,1)S(1)} %get-tuple-element.18), channel_id=1, source_target_pairs={{0,8},{1,24},{2,10},{3,26},{8,0},{9,16},{10,2},{11,18},{16,9},{17,... | collective-permute-start | bytes 98312 | tf_op jit(solution)/shard_map/ppermute | solution.py:340
  15.3 0.0 collective-permute-done.3
  15.3 2.1 %collective-permute-done.4 = bf16[16,1024]{1,0:T(8,128)(2,1)S(1)} collective-permute-done((bf16[16,1024]{1,0:T(8,128)(2,1)S(1)}, bf16[16,1024]{1,0:T(8,128)(2,1)S(1)}, u32[]{:S(2)}, u32[]{:S(2)}) %collective-permute-start.4) | collective-permute-done | bytes 32800 | tf_op jit(solution)/shard_map/ppermute | solution.py:340
  17.4 1.8 %collective-permute-start.6 = (bf16[2,16,1024]{2,1,0:T(8,128)(2,1)S(1)}, bf16[2,16,1024]{2,1,0:T(8,128)(2,1)S(1)}, u32[]{:S(2)}, u32[]{:S(2)}) collective-permute-start(bf16[2,16,1024]{2,1,0:T(8,128)(2,1)S(1)} %get-tuple-element.20), channel_id=1, source_target_pairs={{0,4},{1,5},{2,6},{3,7},{4,0},{5,1},{6,2},{7,3},{8,12},{9,13},{10,... | collective-permute-start | bytes 196616 | tf_op jit(solution)/shard_map/ppermute | solution.py:29
  19.2 0.0 collective-permute-start.5
  19.2 2.9 %collective-permute-start.7 = (bf16[2,16,1024]{2,1,0:T(8,128)(2,1)S(1)}, bf16[2,16,1024]{2,1,0:T(8,128)(2,1)S(1)}, u32[]{:S(2)}, u32[]{:S(2)}) collective-permute-start(bf16[2,16,1024]{2,1,0:T(8,128)(2,1)S(1)} %get-tuple-element.20), channel_id=1, source_target_pairs={{0,6},{1,7},{2,0},{3,1},{4,2},{5,3},{6,4},{7,5},{8,14},{9,15},{10,... | collective-permute-start | bytes 196616 | tf_op jit(solution)/shard_map/ppermute | solution.py:29
  22.1 0.0 collective-permute-done.6
  22.2 2.2 %collective-permute-done.5 = bf16[2,16,1024]{2,1,0:T(8,128)(2,1)S(1)} collective-permute-done((bf16[2,16,1024]{2,1,0:T(8,128)(2,1)S(1)}, bf16[2,16,1024]{2,1,0:T(8,128)(2,1)S(1)}, u32[]{:S(2)}, u32[]{:S(2)}) %collective-permute-start.5) | collective-permute-done | bytes 65568 | tf_op jit(solution)/shard_map/ppermute | solution.py:29
  24.4 0.0 collective-permute-done.7
  24.4 3.8 %collective-permute-start.8 = (bf16[4,2,16,1024]{3,2,1,0:T(8,128)(2,1)S(1)}, bf16[4,2,16,1024]{3,2,1,0:T(8,128)(2,1)S(1)}, u32[]{:S(2)}, u32[]{:S(2)}) collective-permute-start(bf16[4,2,16,1024]{3,2,1,0:T(8,128)(2,1)S(1)} %pad_maximum_fusion.mine_ref), channel_id=1, source_target_pairs={{0,1},{1,0},{2,3},{3,2},{4,5},{5,4},{6,7},{7,6},{8,9},{9,8},{10,11... | collective-permute-start | bytes 786440 | tf_op jit(solution)/shard_map/ppermute | solution.py:345
  28.2 1.2 %collective-permute-done.8.other_ref = bf16[4,2,16,1024]{3,2,1,0:T(8,128)(2,1)S(1)} collective-permute-done((bf16[4,2,16,1024]{3,2,1,0:T(8,128)(2,1)S(1)}, bf16[4,2,16,1024]{3,2,1,0:T(8,128)(2,1)S(1)}, u32[]{:S(2)}, u32[]{:S(2)}) %collective-permute-start.8) | collective-permute-done | bytes 262176 | tf_op jit(solution)/shard_map/ppermute | solution.py:345
  29.4 11.7 %correlate.1 = bf16[2,4,1024,2048]{3,2,1,0:T(8,128)(2,1)} custom-call(bf16[4,2,16,1024]{3,2,1,0:T(8,128)(2,1)S(1)} %pad_maximum_fusion.mine_ref, bf16[4,2,16,1024]{3,2,1,0:T(8,128)(2,1)S(1)} %collective-permute-done.8.other_ref), custom_call_target="tpu_custom_call" | custom-call | tf_op jit(solution)/shard_map/correlate/pallas_call | solution.py:315
  (4 shorter events, 0.1 us)
Async XLA Ops:
  4.2 1.5 %collective-permute-start = (bf16[4,16,1024]{2,1,0:T(8,128)(2,1)S(1)}, bf16[4,16,1024]{2,1,0:T(8,128)(2,1)S(1)}, u32[]{:S(2)}, u32[]{:S(2)}) collective-permute-start(bf16[4,16,1024]{2,1,0:T(8,128)(2,1)S(1)} %get-tuple-element.13), channel_id=1, source_target_pairs={{0,1},{1,0},{2,3},{3,2},{4,5},{5,4},{6,7},{7,6},{8,9},{9,8},{10,11... | collective-permute-start | bytes 393224 | tf_op jit(solution)/shard_map/ppermute | solution.py:345
  5.8 7.0 %collective-permute-start.1 = (bf16[32,1024]{1,0:T(8,128)(2,1)S(1)}, bf16[32,1024]{1,0:T(8,128)(2,1)S(1)}, u32[]{:S(2)}, u32[]{:S(2)}) collective-permute-start(bf16[32,1024]{1,0:T(8,128)(2,1)S(1)} %get-tuple-element.15), channel_id=1, source_target_pairs={{0,2},{1,3},{2,4},{3,5},{4,6},{5,7},{6,0},{7,1},{8,10},{9,11},{10,... | collective-permute-start | bytes 196616 | tf_op jit(solution)/shard_map/ppermute | solution.py:29
  8.7 4.1 %collective-permute-start.2 = (bf16[16,1024]{1,0:T(8,128)(2,1)S(1)}, bf16[16,1024]{1,0:T(8,128)(2,1)S(1)}, u32[]{:S(2)}, u32[]{:S(2)}) collective-permute-start(bf16[16,1024]{1,0:T(8,128)(2,1)S(1)} %get-tuple-element.16), channel_id=1, source_target_pairs={{0,4},{1,5},{2,6},{3,7},{4,0},{5,1},{6,2},{7,3},{8,12},{9,13},{10,... | collective-permute-start | bytes 98312 | tf_op jit(solution)/shard_map/ppermute | solution.py:29
  12.8 2.5 %collective-permute-start.3 = (bf16[16,1024]{1,0:T(8,128)(2,1)S(1)}, bf16[16,1024]{1,0:T(8,128)(2,1)S(1)}, u32[]{:S(2)}, u32[]{:S(2)}) collective-permute-start(bf16[16,1024]{1,0:T(8,128)(2,1)S(1)} %get-tuple-element.17), channel_id=1, source_target_pairs={{0,0},{1,16},{2,2},{3,18},{8,8},{9,24},{10,10},{11,26},{16,1},{17,... | collective-permute-start | bytes 98312 | tf_op jit(solution)/shard_map/ppermute | solution.py:340
  13.5 4.0 %collective-permute-start.4 = (bf16[16,1024]{1,0:T(8,128)(2,1)S(1)}, bf16[16,1024]{1,0:T(8,128)(2,1)S(1)}, u32[]{:S(2)}, u32[]{:S(2)}) collective-permute-start(bf16[16,1024]{1,0:T(8,128)(2,1)S(1)} %get-tuple-element.18), channel_id=1, source_target_pairs={{0,8},{1,24},{2,10},{3,26},{8,0},{9,16},{10,2},{11,18},{16,9},{17,... | collective-permute-start | bytes 98312 | tf_op jit(solution)/shard_map/ppermute | solution.py:340
  17.4 4.7 %collective-permute-start.6 = (bf16[2,16,1024]{2,1,0:T(8,128)(2,1)S(1)}, bf16[2,16,1024]{2,1,0:T(8,128)(2,1)S(1)}, u32[]{:S(2)}, u32[]{:S(2)}) collective-permute-start(bf16[2,16,1024]{2,1,0:T(8,128)(2,1)S(1)} %get-tuple-element.20), channel_id=1, source_target_pairs={{0,4},{1,5},{2,6},{3,7},{4,0},{5,1},{6,2},{7,3},{8,12},{9,13},{10,... | collective-permute-start | bytes 196616 | tf_op jit(solution)/shard_map/ppermute | solution.py:29
  19.2 5.2 %collective-permute-start.5 = (bf16[2,16,1024]{2,1,0:T(8,128)(2,1)S(1)}, bf16[2,16,1024]{2,1,0:T(8,128)(2,1)S(1)}, u32[]{:S(2)}, u32[]{:S(2)}) collective-permute-start(bf16[2,16,1024]{2,1,0:T(8,128)(2,1)S(1)} %get-tuple-element.20), channel_id=1, source_target_pairs={{0,2},{1,3},{2,4},{3,5},{4,6},{5,7},{6,0},{7,1},{8,10},{9,11},{10,... | collective-permute-start | bytes 196616 | tf_op jit(solution)/shard_map/ppermute | solution.py:29
  19.2 5.2 %collective-permute-start.7 = (bf16[2,16,1024]{2,1,0:T(8,128)(2,1)S(1)}, bf16[2,16,1024]{2,1,0:T(8,128)(2,1)S(1)}, u32[]{:S(2)}, u32[]{:S(2)}) collective-permute-start(bf16[2,16,1024]{2,1,0:T(8,128)(2,1)S(1)} %get-tuple-element.20), channel_id=1, source_target_pairs={{0,6},{1,7},{2,0},{3,1},{4,2},{5,3},{6,4},{7,5},{8,14},{9,15},{10,... | collective-permute-start | bytes 196616 | tf_op jit(solution)/shard_map/ppermute | solution.py:29
  24.4 5.0 %collective-permute-start.8 = (bf16[4,2,16,1024]{3,2,1,0:T(8,128)(2,1)S(1)}, bf16[4,2,16,1024]{3,2,1,0:T(8,128)(2,1)S(1)}, u32[]{:S(2)}, u32[]{:S(2)}) collective-permute-start(bf16[4,2,16,1024]{3,2,1,0:T(8,128)(2,1)S(1)} %pad_maximum_fusion.mine_ref), channel_id=1, source_target_pairs={{0,1},{1,0},{2,3},{3,2},{4,5},{5,4},{6,7},{7,6},{8,9},{9,8},{10,11... | collective-permute-start | bytes 786440 | tf_op jit(solution)/shard_map/ppermute | solution.py:345

commit v3 on v2

--- a/solution.py
+++ b/solution.py
@@ -27,6 +27,14 @@
 def rotated(value, axis, by):
     peers = lax.axis_size(axis)
     return lax.ppermute(value, axis, [(i, (i + by) % peers) for i in range(peers)])
+
+
+def plane_steps(planes):
+    assert planes & (planes - 1) == 0 and planes > 1
+    steps = [[], []]
+    for step in reversed(range(planes)):
+        steps[bin(step).count("1") % 2].append(step)
+    return steps
 
 
 def sine_quarter(x):
@@ -52,7 +60,7 @@
 def front_body(
     index_hbm, samples_ref, gr_hbm, gi_hbm, flags_hbm,
     keep_ref, give_ref,
-    index_ref, gr_ref, gi_ref, flags_ref, block_ref, filter_ref, table_ref, acc_ref, sems, small_sems,
+    index_ref, gr_ref, gi_ref, flags_ref, block_ref, filter_ref, table_ref, acc_ref, group_ref, sems, small_sems,
     *, groups,
 ):
     points, width = block_ref.shape
@@ -136,8 +144,9 @@
     gr = jnp.concatenate(gr, 0) * usable
     gi = jnp.concatenate(gi, 0) * usable
     low = lax.rem(lax.broadcasted_iota(jnp.int32, (rows, width), 0), 2 * cg) < cg
-    core = lax.rem(lax.axis_index("row"), 2)
-    half = rows // 2
+    core, plane = lax.rem(lax.axis_index("row"), 2), lax.axis_index("chan")
+    steps = plane_steps(groups)
+    size = 2 * cg
     for k in range(TAPS):
         s = acc_ref[k * rows : (k + 1) * rows]
         if k in PAIR_TAPS:
@@ -145,9 +154,12 @@
             s = s + acc_ref[i * rows : (i + 1) * rows]
         other = jnp.where(low, pltpu.roll(s, rows - cg, 0), pltpu.roll(s, cg, 0))
         volts = gr * s + gi * other
-        first, second = volts[:half], volts[half:]
-        keep_ref[k] = jnp.where(core == 0, first, second)
-        give_ref[k] = jnp.where(core == 0, second, first).astype(give_ref.dtype)
+        for g in range(groups):
+            group_ref[g] = volts[g * size : (g + 1) * size]
+        for i in range(groups // 2):
+            even, odd = group_ref[plane ^ steps[0][i]], group_ref[plane ^ steps[1][i]]
+            keep_ref[k, i * size : (i + 1) * size] = jnp.where(core == 0, even, odd)
+            give_ref[k, i * size : (i + 1) * size] = jnp.where(core == 0, odd, even).astype(give_ref.dtype)
 
 
 def front(samples, channel_index, gain_real, gain_imag, flags, groups):
@@ -174,6 +186,7 @@
             pltpu.VMEM((TAPS, points // LANES, LANES), jnp.float32),
             pltpu.VMEM((depth, points), jnp.bfloat16),
             pltpu.VMEM((depth, width), jnp.float32),
+            pltpu.VMEM((groups, rows // groups, width), jnp.float32),
             pltpu.SemaphoreType.DMA((SPLITS,)),
             pltpu.SemaphoreType.DMA((4,)),
         ],
@@ -214,19 +227,16 @@
 
 def combine_body(here_ref, next_ref, after_ref, *refs):
     out_refs, total_ref = refs[:-1], refs[-1]
-    groups, size, _ = total_ref.shape
-    size = size // 2
+    size = total_ref.shape[0] // 2
     half = after_ref.shape[0]
     chip = lax.axis_index("tm") * (lax.axis_size("row") // 2) + lax.div(lax.axis_index("row"), 2)
     even = here_ref[0] + jnp.where(chip >= 1, next_ref[:half].astype(jnp.float32), 0.0)
     even = even + jnp.where(chip >= 2, after_ref[...].astype(jnp.float32), 0.0)
     odd = here_ref[1] + jnp.where(chip >= 1, next_ref[half:].astype(jnp.float32), 0.0)
-    for g in range(groups):
-        total_ref[g, :size] = even[g * size : (g + 1) * size]
-        total_ref[g, size:] = odd[g * size : (g + 1) * size]
-    me = lax.axis_index("chan")
-    for j, ref in enumerate(out_refs):
-        ref[...] = total_ref[lax.rem(me + j, groups)].astype(jnp.bfloat16)
+    for g, ref in enumerate(out_refs):
+        total_ref[:size] = even[g * size : (g + 1) * size]
+        total_ref[size:] = odd[g * size : (g + 1) * size]
+        ref[...] = total_ref[...].astype(jnp.bfloat16)
 
 
 def combine(here, following, after, groups):
@@ -239,7 +249,7 @@
         out_shape=[piece] * groups,
         in_specs=[IN_VMEM] * 3,
         out_specs=[IN_VMEM] * groups,
-        scratch_shapes=[pltpu.VMEM((groups, size, width), jnp.float32)],
+        scratch_shapes=[pltpu.VMEM((size, width), jnp.float32)],
         compiler_params=pltpu.CompilerParams(vmem_limit_bytes=VMEM_BYTES),
     )(here, following, after)
 
@@ -252,9 +262,10 @@
     frames = 2 * chips
     rows, cols = out_ref.shape[2:]
     core = lax.rem(lax.axis_index("row"), 2)
+    steps = plane_steps(2 * chunks)
     for ref, half in ((mine_ref, core), (other_ref, 1 - core)):
         for j in range(chunks):
-            chunk = half * chunks + lax.rem(lax.axis_index("chan") + chunks - j, chunks)
+            chunk = lax.axis_index("chan") ^ jnp.where(half == 0, steps[0][j], steps[1][j])
             for m in range(chips):
                 all_ref[chunk, m * 2 * size : (m + 1) * 2 * size, :] = ref[m, j].astype(jnp.float32)
     n_row, n_col = rows // width, cols // width
@@ -329,14 +340,10 @@
     )(mine, other)
 
 
-def turn_plane(value, by):
+def turn_plane(value, i):
     planes, rows = lax.axis_size("chan"), lax.axis_size("row")
-    half = planes // 2
-    pairs = []
-    for c in range(planes):
-        for r in range(rows):
-            to = (r % 2) * half + (c + by) % half
-            pairs.append((c * rows + r, to * rows + r - r % 2 + c // half))
+    steps = plane_steps(planes)
+    pairs = [(c * rows + r, (c ^ steps[r % 2][i]) * rows + r) for c in range(planes) for r in range(rows)]
     return lax.ppermute(value, ("chan", "row"), pairs)
 
 
@@ -355,7 +362,8 @@
     after = rotated(after, FRAME_AXES, 4)
     pieces = combine(here, following, after, planes // 2)
     pieces = jnp.stack([turn_plane(piece, j) for j, piece in enumerate(pieces)])
-    mine = jnp.stack([pieces] + [rotated(pieces, FRAME_AXES, 2 * s) for s in range(1, chips)])
+    peers = 2 * chips
+    mine = jnp.stack([pieces] + [lax.ppermute(pieces, FRAME_AXES, [(i, i ^ (2 * s)) for i in range(peers)]) for s in range(1, chips)])
     return correlate(mine, swapped(mine), inputs_total // lax.axis_size("row"), inputs_total // lax.axis_size("tm"))
 
 

time: 41.2 us -> 39.9 us (0.968)
  starting transfers between devices: 16 us -> 13.2 us
  waiting for transfers between devices: 9.08 us -> 10.5 us
    ppermute x5 -> x2, starting transfers between devices: 9.1 us -> 4.4 us  [rotated(): lax.ppermute(value, axis, [(i, (i + by) % peers) for i in range(peers)])]
    ppermute x0 -> x3, waiting for transfers between devices: none -> 4.23 us  [local(): lax.ppermute(pieces, FRAME_AXES, [(i, i ^ 2 * s) for i in range(peers)])]
    ppermute x2, starting transfers between devices: 4.37 us -> 0.74 us  [swapped(): return lax.ppermute(value, FRAME_AXES, [(i, i ^ 1) for i in range(peers)])]
    ppermute x0 -> x3, starting transfers between devices: none -> 3.55 us  [local(): lax.ppermute(pieces, FRAME_AXES, [(i, i ^ 2 * s) for i in range(peers)])]
    ppermute x5 -> x2, waiting for transfers between devices: 4.79 us -> 2.55 us  [rotated(): lax.ppermute(value, axis, [(i, (i + by) % peers) for i in range(peers)])]
    ppermute x2, starting transfers between devices: 2.5 us -> 4.51 us  [turn_plane(): return lax.ppermute(value, ('chan', 'row'), pairs)]
    ppermute x2, waiting for transfers between devices: 2.14 us -> 1.27 us  [turn_plane(): return lax.ppermute(value, ('chan', 'row'), pairs)]
  transfers between devices with their start and end apart: 9 -> 9, of which waited for: 5 -> 7; matrix products, arithmetic and copies ran while one was open for 0% -> 0% of each run, Pallas kernels for 0% -> 0%
where the time goes in v3:
time: 39.9 us; the launch traced here: 39.8 us
  Pallas kernels  16 us (40%)
  starting transfers between devices  13.2 us (33%)
  waiting for transfers between devices  10.5 us (26%)
    pallas_call x1, Pallas kernels, correlate(): pl.pallas_call(functools.partial(correlate_body, tile=TILE), name='correl...  11.7 us
    ppermute x2, starting transfers between devices, turn_plane(): return lax.ppermute(value, ('chan', 'row'), pairs)  4.51 us
    ppermute x2, starting transfers between devices, rotated(): lax.ppermute(value, axis, [(i, (i + by) % peers) for i in range(peers)])  4.4 us
    ppermute x3, waiting for transfers between devices, local(): lax.ppermute(pieces, FRAME_AXES, [(i, i ^ 2 * s) for i in range(peers)])  4.23 us
    pallas_call x1, Pallas kernels, front(): pl.pallas_call(functools.partial(front_body, groups=groups), name='front'...  4.21 us
    ppermute x3, starting transfers between devices, local(): lax.ppermute(pieces, FRAME_AXES, [(i, i ^ 2 * s) for i in range(peers)])  3.55 us
    ppermute x2, waiting for transfers between devices, rotated(): lax.ppermute(value, axis, [(i, (i + by) % peers) for i in range(peers)])  2.55 us
    ppermute x2, waiting for transfers between devices, swapped(): return lax.ppermute(value, FRAME_AXES, [(i, i ^ 1) for i in range(peers)])  2.41 us
  transfers between devices with their start and end apart: 9, of which 7 were waited for; matrix products, arithmetic and copies ran while one was open for 0% of the time, Pallas kernels for 0%

profile of v3, /device:TPU:0, one launch (start us, length us, event | category | flops | bytes accessed | tf_op | source)
XLA Modules:
  0.0 39.8 jit_solution(2671727936263862382)
XLA Ops:
  0.0 4.2 %front.1 = (f32[4,16,1024]{2,1,0:T(8,128)S(1)}, bf16[4,16,1024]{2,1,0:T(8,128)(2,1)S(1)}) custom-call(s32[16]{0:T(128)} %index_hbm.1, bf16[1,4096,1024]{2,1,0:T(8,128)(2,1)} %samples_ref.1, f32[16,1024]{1,0:T(8,128)} %gr_hbm.1, f32[16,1024]{1,0:T(8,128)} %gi_hbm.1, s32[1,512]{1,0:T(1,128)} %bitcast.13), custom_call_target="tpu_custom_call" | custom-call | tf_op jit(solution)/shard_map/front/pallas_call | solution.py:171
  4.2 0.6 %collective-permute-start = (bf16[4,16,1024]{2,1,0:T(8,128)(2,1)S(1)}, bf16[4,16,1024]{2,1,0:T(8,128)(2,1)S(1)}, u32[]{:S(2)}, u32[]{:S(2)}) collective-permute-start(bf16[4,16,1024]{2,1,0:T(8,128)(2,1)S(1)} %get-tuple-element.13), channel_id=1, source_target_pairs={{0,1},{1,0},{2,3},{3,2},{4,5},{5,4},{6,7},{7,6},{8,9},{9,8},{10,11... | collective-permute-start | bytes 393224 | tf_op jit(solution)/shard_map/ppermute | solution.py:352
  4.8 1.0 %collective-permute-done.got_ref = bf16[4,16,1024]{2,1,0:T(8,128)(2,1)S(1)} collective-permute-done((bf16[4,16,1024]{2,1,0:T(8,128)(2,1)S(1)}, bf16[4,16,1024]{2,1,0:T(8,128)(2,1)S(1)}, u32[]{:S(2)}, u32[]{:S(2)}) %collective-permute-start) | collective-permute-done | bytes 131104 | tf_op jit(solution)/shard_map/ppermute | solution.py:352
  5.8 2.9 %collective-permute-start.1 = (bf16[32,1024]{1,0:T(8,128)(2,1)S(1)}, bf16[32,1024]{1,0:T(8,128)(2,1)S(1)}, u32[]{:S(2)}, u32[]{:S(2)}) collective-permute-start(bf16[32,1024]{1,0:T(8,128)(2,1)S(1)} %get-tuple-element.15), channel_id=1, source_target_pairs={{0,2},{1,3},{2,4},{3,5},{4,6},{5,7},{6,0},{7,1},{8,10},{9,11},{10,... | collective-permute-start | bytes 196616 | tf_op jit(solution)/shard_map/ppermute | solution.py:29
  8.7 1.5 %collective-permute-start.2 = (bf16[16,1024]{1,0:T(8,128)(2,1)S(1)}, bf16[16,1024]{1,0:T(8,128)(2,1)S(1)}, u32[]{:S(2)}, u32[]{:S(2)}) collective-permute-start(bf16[16,1024]{1,0:T(8,128)(2,1)S(1)} %get-tuple-element.16), channel_id=1, source_target_pairs={{0,4},{1,5},{2,6},{3,7},{4,0},{5,1},{6,2},{7,3},{8,12},{9,13},{10,... | collective-permute-start | bytes 98312 | tf_op jit(solution)/shard_map/ppermute | solution.py:29
  10.2 2.5 %collective-permute-done.2.after_ref = bf16[16,1024]{1,0:T(8,128)(2,1)S(1)} collective-permute-done((bf16[16,1024]{1,0:T(8,128)(2,1)S(1)}, bf16[16,1024]{1,0:T(8,128)(2,1)S(1)}, u32[]{:S(2)}, u32[]{:S(2)}) %collective-permute-start.2) | collective-permute-done | bytes 32800 | tf_op jit(solution)/shard_map/ppermute | solution.py:29
  12.8 0.0 collective-permute-done.1.next_ref
  12.8 3.9 %collective-permute-start.3 = (bf16[16,1024]{1,0:T(8,128)(2,1)S(1)}, bf16[16,1024]{1,0:T(8,128)(2,1)S(1)}, u32[]{:S(2)}, u32[]{:S(2)}) collective-permute-start(bf16[16,1024]{1,0:T(8,128)(2,1)S(1)} %get-tuple-element.17), channel_id=1, source_target_pairs={{0,24},{1,17},{2,26},{3,19},{8,16},{9,25},{10,18},{11,27},{16,8},{... | collective-permute-start | bytes 98312 | tf_op jit(solution)/shard_map/ppermute | solution.py:347
  16.7 0.7 %collective-permute-start.4 = (bf16[16,1024]{1,0:T(8,128)(2,1)S(1)}, bf16[16,1024]{1,0:T(8,128)(2,1)S(1)}, u32[]{:S(2)}, u32[]{:S(2)}) collective-permute-start(bf16[16,1024]{1,0:T(8,128)(2,1)S(1)} %get-tuple-element.18), channel_id=1, source_target_pairs={{0,0},{1,9},{2,2},{3,11},{8,8},{9,1},{10,10},{11,3},{16,16},{17,25... | collective-permute-start | bytes 98312 | tf_op jit(solution)/shard_map/ppermute | solution.py:347
  17.3 1.3 %collective-permute-done.3 = bf16[16,1024]{1,0:T(8,128)(2,1)S(1)} collective-permute-done((bf16[16,1024]{1,0:T(8,128)(2,1)S(1)}, bf16[16,1024]{1,0:T(8,128)(2,1)S(1)}, u32[]{:S(2)}, u32[]{:S(2)}) %collective-permute-start.3) | collective-permute-done | bytes 32800 | tf_op jit(solution)/shard_map/ppermute | solution.py:347
  18.6 0.0 collective-permute-done.4
  18.6 1.8 %collective-permute-start.6 = (bf16[2,16,1024]{2,1,0:T(8,128)(2,1)S(1)}, bf16[2,16,1024]{2,1,0:T(8,128)(2,1)S(1)}, u32[]{:S(2)}, u32[]{:S(2)}) collective-permute-start(bf16[2,16,1024]{2,1,0:T(8,128)(2,1)S(1)} %get-tuple-element.20), channel_id=1, source_target_pairs={{0,4},{1,5},{2,6},{3,7},{4,0},{5,1},{6,2},{7,3},{8,12},{9,13},{10,... | collective-permute-start | bytes 196616 | tf_op jit(solution)/shard_map/ppermute | solution.py:366
  20.4 0.2 collective-permute-start.5
  20.5 1.6 %collective-permute-start.7 = (bf16[2,16,1024]{2,1,0:T(8,128)(2,1)S(1)}, bf16[2,16,1024]{2,1,0:T(8,128)(2,1)S(1)}, u32[]{:S(2)}, u32[]{:S(2)}) collective-permute-start(bf16[2,16,1024]{2,1,0:T(8,128)(2,1)S(1)} %get-tuple-element.20), channel_id=1, source_target_pairs={{0,6},{1,7},{2,4},{3,5},{4,2},{5,3},{6,0},{7,1},{8,14},{9,15},{10,... | collective-permute-start | bytes 196616 | tf_op jit(solution)/shard_map/ppermute | solution.py:366
  22.2 1.0 %collective-permute-done.6 = bf16[2,16,1024]{2,1,0:T(8,128)(2,1)S(1)} collective-permute-done((bf16[2,16,1024]{2,1,0:T(8,128)(2,1)S(1)}, bf16[2,16,1024]{2,1,0:T(8,128)(2,1)S(1)}, u32[]{:S(2)}, u32[]{:S(2)}) %collective-permute-start.6) | collective-permute-done | bytes 65568 | tf_op jit(solution)/shard_map/ppermute | solution.py:366
  23.2 2.2 %collective-permute-done.5 = bf16[2,16,1024]{2,1,0:T(8,128)(2,1)S(1)} collective-permute-done((bf16[2,16,1024]{2,1,0:T(8,128)(2,1)S(1)}, bf16[2,16,1024]{2,1,0:T(8,128)(2,1)S(1)}, u32[]{:S(2)}, u32[]{:S(2)}) %collective-permute-start.5) | collective-permute-done | bytes 65568 | tf_op jit(solution)/shard_map/ppermute | solution.py:366
  25.3 1.1 %collective-permute-done.7 = bf16[2,16,1024]{2,1,0:T(8,128)(2,1)S(1)} collective-permute-done((bf16[2,16,1024]{2,1,0:T(8,128)(2,1)S(1)}, bf16[2,16,1024]{2,1,0:T(8,128)(2,1)S(1)}, u32[]{:S(2)}, u32[]{:S(2)}) %collective-permute-start.7) | collective-permute-done | bytes 65568 | tf_op jit(solution)/shard_map/ppermute | solution.py:366
  26.4 0.2 collective-permute-start.8
  26.6 1.4 %collective-permute-done.8.other_ref = bf16[4,2,16,1024]{3,2,1,0:T(8,128)(2,1)S(1)} collective-permute-done((bf16[4,2,16,1024]{3,2,1,0:T(8,128)(2,1)S(1)}, bf16[4,2,16,1024]{3,2,1,0:T(8,128)(2,1)S(1)}, u32[]{:S(2)}, u32[]{:S(2)}) %collective-permute-start.8) | collective-permute-done | bytes 262176 | tf_op jit(solution)/shard_map/ppermute | solution.py:352
  28.0 11.7 %correlate.1 = bf16[2,4,1024,2048]{3,2,1,0:T(8,128)(2,1)} custom-call(bf16[4,2,16,1024]{3,2,1,0:T(8,128)(2,1)S(1)} %pad_maximum_fusion.mine_ref, bf16[4,2,16,1024]{3,2,1,0:T(8,128)(2,1)S(1)} %collective-permute-done.8.other_ref), custom_call_target="tpu_custom_call" | custom-call | tf_op jit(solution)/shard_map/correlate/pallas_call | solution.py:326
  (4 shorter events, 0.1 us)
Async XLA Ops:
  4.2 1.5 %collective-permute-start = (bf16[4,16,1024]{2,1,0:T(8,128)(2,1)S(1)}, bf16[4,16,1024]{2,1,0:T(8,128)(2,1)S(1)}, u32[]{:S(2)}, u32[]{:S(2)}) collective-permute-start(bf16[4,16,1024]{2,1,0:T(8,128)(2,1)S(1)} %get-tuple-element.13), channel_id=1, source_target_pairs={{0,1},{1,0},{2,3},{3,2},{4,5},{5,4},{6,7},{7,6},{8,9},{9,8},{10,11... | collective-permute-start | bytes 393224 | tf_op jit(solution)/shard_map/ppermute | solution.py:352
  5.8 7.0 %collective-permute-start.1 = (bf16[32,1024]{1,0:T(8,128)(2,1)S(1)}, bf16[32,1024]{1,0:T(8,128)(2,1)S(1)}, u32[]{:S(2)}, u32[]{:S(2)}) collective-permute-start(bf16[32,1024]{1,0:T(8,128)(2,1)S(1)} %get-tuple-element.15), channel_id=1, source_target_pairs={{0,2},{1,3},{2,4},{3,5},{4,6},{5,7},{6,0},{7,1},{8,10},{9,11},{10,... | collective-permute-start | bytes 196616 | tf_op jit(solution)/shard_map/ppermute | solution.py:29
  8.7 4.1 %collective-permute-start.2 = (bf16[16,1024]{1,0:T(8,128)(2,1)S(1)}, bf16[16,1024]{1,0:T(8,128)(2,1)S(1)}, u32[]{:S(2)}, u32[]{:S(2)}) collective-permute-start(bf16[16,1024]{1,0:T(8,128)(2,1)S(1)} %get-tuple-element.16), channel_id=1, source_target_pairs={{0,4},{1,5},{2,6},{3,7},{4,0},{5,1},{6,2},{7,3},{8,12},{9,13},{10,... | collective-permute-start | bytes 98312 | tf_op jit(solution)/shard_map/ppermute | solution.py:29
  12.8 5.8 %collective-permute-start.3 = (bf16[16,1024]{1,0:T(8,128)(2,1)S(1)}, bf16[16,1024]{1,0:T(8,128)(2,1)S(1)}, u32[]{:S(2)}, u32[]{:S(2)}) collective-permute-start(bf16[16,1024]{1,0:T(8,128)(2,1)S(1)} %get-tuple-element.17), channel_id=1, source_target_pairs={{0,24},{1,17},{2,26},{3,19},{8,16},{9,25},{10,18},{11,27},{16,8},{... | collective-permute-start | bytes 98312 | tf_op jit(solution)/shard_map/ppermute | solution.py:347
  16.7 1.9 %collective-permute-start.4 = (bf16[16,1024]{1,0:T(8,128)(2,1)S(1)}, bf16[16,1024]{1,0:T(8,128)(2,1)S(1)}, u32[]{:S(2)}, u32[]{:S(2)}) collective-permute-start(bf16[16,1024]{1,0:T(8,128)(2,1)S(1)} %get-tuple-element.18), channel_id=1, source_target_pairs={{0,0},{1,9},{2,2},{3,11},{8,8},{9,1},{10,10},{11,3},{16,16},{17,25... | collective-permute-start | bytes 98312 | tf_op jit(solution)/shard_map/ppermute | solution.py:347
  18.6 4.6 %collective-permute-start.6 = (bf16[2,16,1024]{2,1,0:T(8,128)(2,1)S(1)}, bf16[2,16,1024]{2,1,0:T(8,128)(2,1)S(1)}, u32[]{:S(2)}, u32[]{:S(2)}) collective-permute-start(bf16[2,16,1024]{2,1,0:T(8,128)(2,1)S(1)} %get-tuple-element.20), channel_id=1, source_target_pairs={{0,4},{1,5},{2,6},{3,7},{4,0},{5,1},{6,2},{7,3},{8,12},{9,13},{10,... | collective-permute-start | bytes 196616 | tf_op jit(solution)/shard_map/ppermute | solution.py:366
  20.4 5.0 %collective-permute-start.5 = (bf16[2,16,1024]{2,1,0:T(8,128)(2,1)S(1)}, bf16[2,16,1024]{2,1,0:T(8,128)(2,1)S(1)}, u32[]{:S(2)}, u32[]{:S(2)}) collective-permute-start(bf16[2,16,1024]{2,1,0:T(8,128)(2,1)S(1)} %get-tuple-element.20), channel_id=1, source_target_pairs={{0,2},{1,3},{2,0},{3,1},{4,6},{5,7},{6,4},{7,5},{8,10},{9,11},{10,... | collective-permute-start | bytes 196616 | tf_op jit(solution)/shard_map/ppermute | solution.py:366
  20.5 5.9 %collective-permute-start.7 = (bf16[2,16,1024]{2,1,0:T(8,128)(2,1)S(1)}, bf16[2,16,1024]{2,1,0:T(8,128)(2,1)S(1)}, u32[]{:S(2)}, u32[]{:S(2)}) collective-permute-start(bf16[2,16,1024]{2,1,0:T(8,128)(2,1)S(1)} %get-tuple-element.20), channel_id=1, source_target_pairs={{0,6},{1,7},{2,4},{3,5},{4,2},{5,3},{6,0},{7,1},{8,14},{9,15},{10,... | collective-permute-start | bytes 196616 | tf_op jit(solution)/shard_map/ppermute | solution.py:366
  26.4 1.6 %collective-permute-start.8 = (bf16[4,2,16,1024]{3,2,1,0:T(8,128)(2,1)S(1)}, bf16[4,2,16,1024]{3,2,1,0:T(8,128)(2,1)S(1)}, u32[]{:S(2)}, u32[]{:S(2)}) collective-permute-start(bf16[4,2,16,1024]{3,2,1,0:T(8,128)(2,1)S(1)} %pad_maximum_fusion.mine_ref), channel_id=1, source_target_pairs={{0,1},{1,0},{2,3},{3,2},{4,5},{5,4},{6,7},{7,6},{8,9},{9,8},{10,11... | collective-permute-start | bytes 786440 | tf_op jit(solution)/shard_map/ppermute | solution.py:352

commit v4 on v3

--- a/solution.py
+++ b/solution.py
@@ -35,6 +35,11 @@
     for step in reversed(range(planes)):
         steps[bin(step).count("1") % 2].append(step)
     return steps
+
+
+def chunk_of(plane, core, i, steps):
+    even, odd = steps[0][i], steps[1][i]
+    return plane ^ jnp.where(((core ^ plane ^ even) & 1) == 0, even, odd)
 
 
 def sine_quarter(x):
@@ -254,18 +259,21 @@
     )(here, following, after)
 
 
-def correlate_body(mine_ref, other_ref, out_ref, all_ref, left_ref, right_ref, tile_ref, sems, *, tile):
+def correlate_body(*refs, phase, tile):
+    mine_ref, other_ref = refs[0], refs[1]
+    out_ref, all_ref, left_ref, right_ref, tile_ref, sems = refs[-6:]
     chips, chunks, size, width = mine_ref.shape
     depth = chips * size
     size = size // 2
     cg = size // 2
     frames = 2 * chips
-    rows, cols = out_ref.shape[2:]
-    core = lax.rem(lax.axis_index("row"), 2)
+    rows = out_ref.shape[2]
+    cols = tile_ref.shape[3]
+    core, plane = lax.rem(lax.axis_index("row"), 2), lax.axis_index("chan")
     steps = plane_steps(2 * chunks)
-    for ref, half in ((mine_ref, core), (other_ref, 1 - core)):
+    for ref, half in ((mine_ref, core),) + (() if phase == 0 else ((other_ref, 1 - core),)):
         for j in range(chunks):
-            chunk = lax.axis_index("chan") ^ jnp.where(half == 0, steps[0][j], steps[1][j])
+            chunk = chunk_of(plane, half, j, steps)
             for m in range(chips):
                 all_ref[chunk, m * 2 * size : (m + 1) * 2 * size, :] = ref[m, j].astype(jnp.float32)
     n_row, n_col = rows // width, cols // width
@@ -275,9 +283,11 @@
         for c in range(cg):
             mine = jnp.where(lax.rem(lane, cg) == c, turned, 0.0)
             left_ref[c, q * width : (q + 1) * width, :] = mine.astype(jnp.bfloat16)
+    shift = {None: 0, 0: core, 1: 1 - core}[phase]
+    first = lax.axis_index("tm") * (out_ref.shape[3] // width) + shift
     low = lax.rem(lax.broadcasted_iota(jnp.int32, (depth, width), 0), size) < cg
     for q in range(n_col):
-        x = all_ref[lax.axis_index("tm") * n_col + q]
+        x = all_ref[first + q]
         part = slice(q * width, (q + 1) * width)
         right_ref[0, :, part] = x.astype(jnp.bfloat16)
         crossed = jnp.where(low, -pltpu.roll(x, depth - cg, 0), pltpu.roll(x, cg, 0))
@@ -285,65 +295,73 @@
 
     high, wide = min(tile, rows), min(tile, cols)
     spots = [(top, left) for left in range(0, cols, wide) for top in range(0, rows, high)]
-    total = 2 * cg
-
-    def copy(n, s):
+
+    slots = tile_ref.shape[0]
+
+    def copy(ri, c, s):
         top, left = spots[s]
-        slot = lax.rem(n, 2)
+        slot = c % slots
         return pltpu.make_async_copy(
-            tile_ref.at[slot, pl.ds(top, high), pl.ds(left, wide)],
-            out_ref.at[lax.rem(n, 2), lax.div(n, 2), pl.ds(top, high), pl.ds(left, wide)],
-            sems.at[slot, s],
+            tile_ref.at[slot, ri, pl.ds(top, high), pl.ds(left, wide)],
+            out_ref.at[ri, c, pl.ds(top, high), pl.ds(pl.multiple_of(shift * width + left, wide), wide)],
+            sems.at[slot, ri, s],
         )
 
-    def step(n, carry):
-        @pl.when(n >= 2)
-        def _():
+    def step(c, carry):
+        if c >= slots:
+            for ri in range(2):
+                for s in range(len(spots)):
+                    copy(ri, c - slots, s).wait()
+
+        for ri in range(2):
+            for s, (top, left) in enumerate(spots):
+                product = jnp.dot(
+                    left_ref[c, top : top + high, :],
+                    right_ref[ri, :, left : left + wide],
+                    preferred_element_type=jnp.float32,
+                )
+                tile_ref[c % slots, ri, top : top + high, left : left + wide] = product.astype(jnp.bfloat16)
+                copy(ri, c, s).start()
+
+    for c in range(cg):
+        step(c, 0)
+    for c in range(max(cg - slots, 0), cg):
+        for ri in range(2):
             for s in range(len(spots)):
-                copy(n - 2, s).wait()
-
-        for s, (top, left) in enumerate(spots):
-            product = jnp.dot(
-                left_ref[lax.div(n, 2), top : top + high, :],
-                right_ref[lax.rem(n, 2), :, left : left + wide],
-                preferred_element_type=jnp.float32,
-            )
-            tile_ref[lax.rem(n, 2), top : top + high, left : left + wide] = product.astype(jnp.bfloat16)
-            copy(n, s).start()
-        return carry
-
-    lax.fori_loop(0, total, step, 0)
-    for n in range(total - 2, total):
-        for s in range(len(spots)):
-            copy(n, s).wait()
-
-
-def correlate(mine, other, rows, cols):
-    chips, chunks, size, width = mine.shape
+                copy(ri, c, s).wait()
+
+
+def correlate(operands, rows, cols, phase):
+    chips, chunks, size, width = operands[0].shape
     cg = size // 4
     depth = chips * size
-    spots = (rows // min(TILE, rows)) * (cols // min(TILE, cols))
+    span = cols if phase is None else width
+    spots = (rows // min(TILE, rows)) * (span // min(TILE, span))
     return pl.pallas_call(
-        functools.partial(correlate_body, tile=TILE),
-        name="correlate",
+        functools.partial(correlate_body, phase=phase, tile=TILE),
+        name="correlate" if phase is None else ("correlate_near", "correlate_far")[phase],
         out_shape=jax.ShapeDtypeStruct((2, cg, rows, cols), jnp.bfloat16),
-        in_specs=[IN_VMEM] * 2,
+        in_specs=[IN_VMEM] * min(len(operands), 2) + [IN_HBM] * (len(operands) - 2),
         out_specs=IN_HBM,
+        input_output_aliases={2: 0} if phase == 1 else {},
         scratch_shapes=[
             pltpu.VMEM((2 * chunks, depth, width), jnp.float32),
             pltpu.VMEM((cg, rows, depth), jnp.bfloat16),
-            pltpu.VMEM((2, depth, cols), jnp.bfloat16),
-            pltpu.VMEM((2, rows, cols), jnp.bfloat16),
-            pltpu.SemaphoreType.DMA((2, spots)),
+            pltpu.VMEM((2, depth, span), jnp.bfloat16),
+            pltpu.VMEM((2, 2, rows, span), jnp.bfloat16),
+            pltpu.SemaphoreType.DMA((2, 2, spots)),
         ],
         compiler_params=pltpu.CompilerParams(vmem_limit_bytes=VMEM_BYTES),
-    )(mine, other)
+    )(*operands)
 
 
 def turn_plane(value, i):
     planes, rows = lax.axis_size("chan"), lax.axis_size("row")
     steps = plane_steps(planes)
-    pairs = [(c * rows + r, (c ^ steps[r % 2][i]) * rows + r) for c in range(planes) for r in range(rows)]
+    pairs = []
+    for c in range(planes):
+        for r in range(rows):
+            pairs.append((c * rows + r, (c ^ steps[r % 2][i]) * rows + r - r % 2 + c % 2))
     return lax.ppermute(value, ("chan", "row"), pairs)
 
 
@@ -358,13 +376,19 @@
     inputs_total = samples.shape[2] * planes
     keep, give = front(samples, channel_index, gain_real, gain_imag, flags, planes)
     here, following, after = pair_sum(keep, swapped(give))
+    after = rotated(after, FRAME_AXES, 4)
     following = rotated(following, FRAME_AXES, 2)
-    after = rotated(after, FRAME_AXES, 4)
     pieces = combine(here, following, after, planes // 2)
     pieces = jnp.stack([turn_plane(piece, j) for j, piece in enumerate(pieces)])
     peers = 2 * chips
     mine = jnp.stack([pieces] + [lax.ppermute(pieces, FRAME_AXES, [(i, i ^ (2 * s)) for i in range(peers)]) for s in range(1, chips)])
-    return correlate(mine, swapped(mine), inputs_total // lax.axis_size("row"), inputs_total // lax.axis_size("tm"))
+    other = swapped(mine)
+    rows, cols = inputs_total // lax.axis_size("row"), inputs_total // lax.axis_size("tm")
+    width = samples.shape[2]
+    if rows != width or cols != 2 * width:
+        return correlate([mine, other], rows, cols, None)
+    near = correlate([mine], rows, cols, 0)
+    return correlate([mine, other, near], rows, cols, 1)
 
 
 def solution(mesh):

time: 39.9 us -> 39.4 us (0.987)
  waiting for transfers between devices: 10.5 us -> 8.33 us
  Pallas kernels: 16 us -> 17 us
  starting transfers between devices: 13.2 us -> 13.6 us
    ppermute x2, waiting for transfers between devices: 2.41 us -> 0.99 us  [swapped(): return lax.ppermute(value, FRAME_AXES, [(i, i ^ 1) for i in range(peers)])]
    pallas_call x1 -> x2, Pallas kernels: 11.7 us -> 12.7 us  [correlate(): pl.pallas_call(functools.partial(correlate_body, phase=phase, tile=TILE),...]
    ppermute x2, waiting for transfers between devices: 1.27 us -> 0.76 us  [turn_plane(): return lax.ppermute(value, ('chan', 'row'), pairs)]
  transfers between devices with their start and end apart: 9 -> 9, of which waited for: 7 -> 6; matrix products, arithmetic and copies ran while one was open for 0% -> 0% of each run, Pallas kernels for 0% -> 16%
where the time goes in v4:
time: 39.4 us; the launch traced here: 39.2 us
  Pallas kernels  17 us (43%)
  starting transfers between devices  13.6 us (35%)
  waiting for transfers between devices  8.33 us (21%)
    pallas_call x2, Pallas kernels, correlate(): pl.pallas_call(functools.partial(correlate_body, phase=phase, tile=TILE),...  12.7 us
    ppermute x2, starting transfers between devices, turn_plane(): return lax.ppermute(value, ('chan', 'row'), pairs)  4.67 us
    ppermute x2, starting transfers between devices, rotated(): lax.ppermute(value, axis, [(i, (i + by) % peers) for i in range(peers)])  4.41 us
    pallas_call x1, Pallas kernels, front(): pl.pallas_call(functools.partial(front_body, groups=groups), name='front'...  4.21 us
    ppermute x3, waiting for transfers between devices, local(): lax.ppermute(pieces, FRAME_AXES, [(i, i ^ 2 * s) for i in range(peers)])  4.03 us
    ppermute x3, starting transfers between devices, local(): lax.ppermute(pieces, FRAME_AXES, [(i, i ^ 2 * s) for i in range(peers)])  3.55 us
    ppermute x2, waiting for transfers between devices, rotated(): lax.ppermute(value, axis, [(i, (i + by) % peers) for i in range(peers)])  2.55 us
    ppermute x2, waiting for transfers between devices, swapped(): return lax.ppermute(value, FRAME_AXES, [(i, i ^ 1) for i in range(peers)])  0.99 us
  transfers between devices with their start and end apart: 9, of which 6 were waited for; matrix products, arithmetic and copies ran while one was open for 0% of the time, Pallas kernels for 16%

profile of v4, /device:TPU:0, one launch (start us, length us, event | category | flops | bytes accessed | tf_op | source)
XLA Modules:
  0.0 39.2 jit_solution(15304866333974770862)
XLA Ops:
  0.0 4.2 %front.1 = (f32[4,16,1024]{2,1,0:T(8,128)S(1)}, bf16[4,16,1024]{2,1,0:T(8,128)(2,1)S(1)}) custom-call(s32[16]{0:T(128)} %index_hbm.1, bf16[1,4096,1024]{2,1,0:T(8,128)(2,1)} %samples_ref.1, f32[16,1024]{1,0:T(8,128)} %gr_hbm.1, f32[16,1024]{1,0:T(8,128)} %gi_hbm.1, s32[1,512]{1,0:T(1,128)} %bitcast.13), custom_call_target="tpu_custom_call" | custom-call | tf_op jit(solution)/shard_map/front/pallas_call | solution.py:176
  4.2 0.6 %collective-permute-start = (bf16[4,16,1024]{2,1,0:T(8,128)(2,1)S(1)}, bf16[4,16,1024]{2,1,0:T(8,128)(2,1)S(1)}, u32[]{:S(2)}, u32[]{:S(2)}) collective-permute-start(bf16[4,16,1024]{2,1,0:T(8,128)(2,1)S(1)} %get-tuple-element.13), channel_id=1, source_target_pairs={{0,1},{1,0},{2,3},{3,2},{4,5},{5,4},{6,7},{7,6},{8,9},{9,8},{10,11... | collective-permute-start | bytes 393224 | tf_op jit(solution)/shard_map/ppermute | solution.py:370
  4.8 1.0 %collective-permute-done.got_ref = bf16[4,16,1024]{2,1,0:T(8,128)(2,1)S(1)} collective-permute-done((bf16[4,16,1024]{2,1,0:T(8,128)(2,1)S(1)}, bf16[4,16,1024]{2,1,0:T(8,128)(2,1)S(1)}, u32[]{:S(2)}, u32[]{:S(2)}) %collective-permute-start) | collective-permute-done | bytes 131104 | tf_op jit(solution)/shard_map/ppermute | solution.py:370
  5.8 2.9 %collective-permute-start.1 = (bf16[32,1024]{1,0:T(8,128)(2,1)S(1)}, bf16[32,1024]{1,0:T(8,128)(2,1)S(1)}, u32[]{:S(2)}, u32[]{:S(2)}) collective-permute-start(bf16[32,1024]{1,0:T(8,128)(2,1)S(1)} %get-tuple-element.15), channel_id=1, source_target_pairs={{0,2},{1,3},{2,4},{3,5},{4,6},{5,7},{6,0},{7,1},{8,10},{9,11},{10,... | collective-permute-start | bytes 196616 | tf_op jit(solution)/shard_map/ppermute | solution.py:29
  8.7 1.5 %collective-permute-start.2 = (bf16[16,1024]{1,0:T(8,128)(2,1)S(1)}, bf16[16,1024]{1,0:T(8,128)(2,1)S(1)}, u32[]{:S(2)}, u32[]{:S(2)}) collective-permute-start(bf16[16,1024]{1,0:T(8,128)(2,1)S(1)} %get-tuple-element.16), channel_id=1, source_target_pairs={{0,4},{1,5},{2,6},{3,7},{4,0},{5,1},{6,2},{7,3},{8,12},{9,13},{10,... | collective-permute-start | bytes 98312 | tf_op jit(solution)/shard_map/ppermute | solution.py:29
  10.2 2.5 %collective-permute-done.2.after_ref = bf16[16,1024]{1,0:T(8,128)(2,1)S(1)} collective-permute-done((bf16[16,1024]{1,0:T(8,128)(2,1)S(1)}, bf16[16,1024]{1,0:T(8,128)(2,1)S(1)}, u32[]{:S(2)}, u32[]{:S(2)}) %collective-permute-start.2) | collective-permute-done | bytes 32800 | tf_op jit(solution)/shard_map/ppermute | solution.py:29
  12.8 0.0 collective-permute-done.1.next_ref
  12.8 3.8 %collective-permute-start.3 = (bf16[16,1024]{1,0:T(8,128)(2,1)S(1)}, bf16[16,1024]{1,0:T(8,128)(2,1)S(1)}, u32[]{:S(2)}, u32[]{:S(2)}) collective-permute-start(bf16[16,1024]{1,0:T(8,128)(2,1)S(1)} %get-tuple-element.17), channel_id=1, source_target_pairs={{0,24},{1,16},{2,26},{3,18},{8,17},{9,25},{10,19},{11,27},{16,8},{... | collective-permute-start | bytes 98312 | tf_op jit(solution)/shard_map/ppermute | solution.py:365
  16.7 0.8 %collective-permute-start.4 = (bf16[16,1024]{1,0:T(8,128)(2,1)S(1)}, bf16[16,1024]{1,0:T(8,128)(2,1)S(1)}, u32[]{:S(2)}, u32[]{:S(2)}) collective-permute-start(bf16[16,1024]{1,0:T(8,128)(2,1)S(1)} %get-tuple-element.18), channel_id=1, source_target_pairs={{0,0},{1,8},{2,2},{3,10},{8,9},{9,1},{10,11},{11,3},{16,16},{17,24... | collective-permute-start | bytes 98312 | tf_op jit(solution)/shard_map/ppermute | solution.py:365
  17.5 0.8 %collective-permute-done.3 = bf16[16,1024]{1,0:T(8,128)(2,1)S(1)} collective-permute-done((bf16[16,1024]{1,0:T(8,128)(2,1)S(1)}, bf16[16,1024]{1,0:T(8,128)(2,1)S(1)}, u32[]{:S(2)}, u32[]{:S(2)}) %collective-permute-start.3) | collective-permute-done | bytes 32800 | tf_op jit(solution)/shard_map/ppermute | solution.py:365
  18.3 0.0 collective-permute-done.4
  18.3 1.6 %collective-permute-start.6 = (bf16[2,16,1024]{2,1,0:T(8,128)(2,1)S(1)}, bf16[2,16,1024]{2,1,0:T(8,128)(2,1)S(1)}, u32[]{:S(2)}, u32[]{:S(2)}) collective-permute-start(bf16[2,16,1024]{2,1,0:T(8,128)(2,1)S(1)} %get-tuple-element.20), channel_id=1, source_target_pairs={{0,4},{1,5},{2,6},{3,7},{4,0},{5,1},{6,2},{7,3},{8,12},{9,13},{10,... | collective-permute-start | bytes 196616 | tf_op jit(solution)/shard_map/ppermute | solution.py:384
  19.9 0.1 collective-permute-start.5
  20.0 1.8 %collective-permute-start.7 = (bf16[2,16,1024]{2,1,0:T(8,128)(2,1)S(1)}, bf16[2,16,1024]{2,1,0:T(8,128)(2,1)S(1)}, u32[]{:S(2)}, u32[]{:S(2)}) collective-permute-start(bf16[2,16,1024]{2,1,0:T(8,128)(2,1)S(1)} %get-tuple-element.20), channel_id=1, source_target_pairs={{0,6},{1,7},{2,4},{3,5},{4,2},{5,3},{6,0},{7,1},{8,14},{9,15},{10,... | collective-permute-start | bytes 196616 | tf_op jit(solution)/shard_map/ppermute | solution.py:384
  21.8 0.8 %collective-permute-done.6 = bf16[2,16,1024]{2,1,0:T(8,128)(2,1)S(1)} collective-permute-done((bf16[2,16,1024]{2,1,0:T(8,128)(2,1)S(1)}, bf16[2,16,1024]{2,1,0:T(8,128)(2,1)S(1)}, u32[]{:S(2)}, u32[]{:S(2)}) %collective-permute-start.6) | collective-permute-done | bytes 65568 | tf_op jit(solution)/shard_map/ppermute | solution.py:384
  22.6 1.5 %collective-permute-done.5 = bf16[2,16,1024]{2,1,0:T(8,128)(2,1)S(1)} collective-permute-done((bf16[2,16,1024]{2,1,0:T(8,128)(2,1)S(1)}, bf16[2,16,1024]{2,1,0:T(8,128)(2,1)S(1)}, u32[]{:S(2)}, u32[]{:S(2)}) %collective-permute-start.5) | collective-permute-done | bytes 65568 | tf_op jit(solution)/shard_map/ppermute | solution.py:384
  24.1 1.7 %collective-permute-done.7 = bf16[2,16,1024]{2,1,0:T(8,128)(2,1)S(1)} collective-permute-done((bf16[2,16,1024]{2,1,0:T(8,128)(2,1)S(1)}, bf16[2,16,1024]{2,1,0:T(8,128)(2,1)S(1)}, u32[]{:S(2)}, u32[]{:S(2)}) %collective-permute-start.7) | collective-permute-done | bytes 65568 | tf_op jit(solution)/shard_map/ppermute | solution.py:384
  25.9 0.4 %collective-permute-start.8 = (bf16[4,2,16,1024]{3,2,1,0:T(8,128)(2,1)S(1)}, bf16[4,2,16,1024]{3,2,1,0:T(8,128)(2,1)S(1)}, u32[]{:S(2)}, u32[]{:S(2)}) collective-permute-start(bf16[4,2,16,1024]{3,2,1,0:T(8,128)(2,1)S(1)} %pad_maximum_fusion.refs_0_), channel_id=1, source_target_pairs={{0,1},{1,0},{2,3},{3,2},{4,5},{5,4},{6,7},{7,6},{8,9},{9,8},{10,11... | collective-permute-start | bytes 786440 | tf_op jit(solution)/shard_map/ppermute | solution.py:370
  26.3 6.3 %correlate_near.1.refs_2_ = bf16[2,4,1024,2048]{3,2,1,0:T(8,128)(2,1)} custom-call(bf16[4,2,16,1024]{3,2,1,0:T(8,128)(2,1)S(1)} %pad_maximum_fusion.refs_0_), custom_call_target="tpu_custom_call" | custom-call | tf_op jit(solution)/shard_map/correlate_near/pallas_call | solution.py:340
  32.6 0.0 collective-permute-done.8.refs_1_
  32.7 6.4 %correlate_far.1 = bf16[2,4,1024,2048]{3,2,1,0:T(8,128)(2,1)} custom-call(bf16[4,2,16,1024]{3,2,1,0:T(8,128)(2,1)S(1)} %pad_maximum_fusion.refs_0_, bf16[4,2,16,1024]{3,2,1,0:T(8,128)(2,1)S(1)} %collective-permute-done.8.refs_1_, bf16[2,4,1024,2048]{3,2,1,0:T(8,128)(2,1)} %correlate_near.1.refs_2_), custom_call_target="tpu_custom_call", output_to_operand_aliasing={{}: (2, {})} | custom-call | tf_op jit(solution)/shard_map/correlate_far/pallas_call | solution.py:340
  (4 shorter events, 0.1 us)
Async XLA Ops:
  4.2 1.5 %collective-permute-start = (bf16[4,16,1024]{2,1,0:T(8,128)(2,1)S(1)}, bf16[4,16,1024]{2,1,0:T(8,128)(2,1)S(1)}, u32[]{:S(2)}, u32[]{:S(2)}) collective-permute-start(bf16[4,16,1024]{2,1,0:T(8,128)(2,1)S(1)} %get-tuple-element.13), channel_id=1, source_target_pairs={{0,1},{1,0},{2,3},{3,2},{4,5},{5,4},{6,7},{7,6},{8,9},{9,8},{10,11... | collective-permute-start | bytes 393224 | tf_op jit(solution)/shard_map/ppermute | solution.py:370
  5.8 7.0 %collective-permute-start.1 = (bf16[32,1024]{1,0:T(8,128)(2,1)S(1)}, bf16[32,1024]{1,0:T(8,128)(2,1)S(1)}, u32[]{:S(2)}, u32[]{:S(2)}) collective-permute-start(bf16[32,1024]{1,0:T(8,128)(2,1)S(1)} %get-tuple-element.15), channel_id=1, source_target_pairs={{0,2},{1,3},{2,4},{3,5},{4,6},{5,7},{6,0},{7,1},{8,10},{9,11},{10,... | collective-permute-start | bytes 196616 | tf_op jit(solution)/shard_map/ppermute | solution.py:29
  8.7 4.1 %collective-permute-start.2 = (bf16[16,1024]{1,0:T(8,128)(2,1)S(1)}, bf16[16,1024]{1,0:T(8,128)(2,1)S(1)}, u32[]{:S(2)}, u32[]{:S(2)}) collective-permute-start(bf16[16,1024]{1,0:T(8,128)(2,1)S(1)} %get-tuple-element.16), channel_id=1, source_target_pairs={{0,4},{1,5},{2,6},{3,7},{4,0},{5,1},{6,2},{7,3},{8,12},{9,13},{10,... | collective-permute-start | bytes 98312 | tf_op jit(solution)/shard_map/ppermute | solution.py:29
  12.8 5.4 %collective-permute-start.3 = (bf16[16,1024]{1,0:T(8,128)(2,1)S(1)}, bf16[16,1024]{1,0:T(8,128)(2,1)S(1)}, u32[]{:S(2)}, u32[]{:S(2)}) collective-permute-start(bf16[16,1024]{1,0:T(8,128)(2,1)S(1)} %get-tuple-element.17), channel_id=1, source_target_pairs={{0,24},{1,16},{2,26},{3,18},{8,17},{9,25},{10,19},{11,27},{16,8},{... | collective-permute-start | bytes 98312 | tf_op jit(solution)/shard_map/ppermute | solution.py:365
  16.7 1.6 %collective-permute-start.4 = (bf16[16,1024]{1,0:T(8,128)(2,1)S(1)}, bf16[16,1024]{1,0:T(8,128)(2,1)S(1)}, u32[]{:S(2)}, u32[]{:S(2)}) collective-permute-start(bf16[16,1024]{1,0:T(8,128)(2,1)S(1)} %get-tuple-element.18), channel_id=1, source_target_pairs={{0,0},{1,8},{2,2},{3,10},{8,9},{9,1},{10,11},{11,3},{16,16},{17,24... | collective-permute-start | bytes 98312 | tf_op jit(solution)/shard_map/ppermute | solution.py:365
  18.3 4.3 %collective-permute-start.6 = (bf16[2,16,1024]{2,1,0:T(8,128)(2,1)S(1)}, bf16[2,16,1024]{2,1,0:T(8,128)(2,1)S(1)}, u32[]{:S(2)}, u32[]{:S(2)}) collective-permute-start(bf16[2,16,1024]{2,1,0:T(8,128)(2,1)S(1)} %get-tuple-element.20), channel_id=1, source_target_pairs={{0,4},{1,5},{2,6},{3,7},{4,0},{5,1},{6,2},{7,3},{8,12},{9,13},{10,... | collective-permute-start | bytes 196616 | tf_op jit(solution)/shard_map/ppermute | solution.py:384
  19.9 4.3 %collective-permute-start.5 = (bf16[2,16,1024]{2,1,0:T(8,128)(2,1)S(1)}, bf16[2,16,1024]{2,1,0:T(8,128)(2,1)S(1)}, u32[]{:S(2)}, u32[]{:S(2)}) collective-permute-start(bf16[2,16,1024]{2,1,0:T(8,128)(2,1)S(1)} %get-tuple-element.20), channel_id=1, source_target_pairs={{0,2},{1,3},{2,0},{3,1},{4,6},{5,7},{6,4},{7,5},{8,10},{9,11},{10,... | collective-permute-start | bytes 196616 | tf_op jit(solution)/shard_map/ppermute | solution.py:384
  20.0 5.9 %collective-permute-start.7 = (bf16[2,16,1024]{2,1,0:T(8,128)(2,1)S(1)}, bf16[2,16,1024]{2,1,0:T(8,128)(2,1)S(1)}, u32[]{:S(2)}, u32[]{:S(2)}) collective-permute-start(bf16[2,16,1024]{2,1,0:T(8,128)(2,1)S(1)} %get-tuple-element.20), channel_id=1, source_target_pairs={{0,6},{1,7},{2,4},{3,5},{4,2},{5,3},{6,0},{7,1},{8,14},{9,15},{10,... | collective-permute-start | bytes 196616 | tf_op jit(solution)/shard_map/ppermute | solution.py:384
  25.9 6.7 %collective-permute-start.8 = (bf16[4,2,16,1024]{3,2,1,0:T(8,128)(2,1)S(1)}, bf16[4,2,16,1024]{3,2,1,0:T(8,128)(2,1)S(1)}, u32[]{:S(2)}, u32[]{:S(2)}) collective-permute-start(bf16[4,2,16,1024]{3,2,1,0:T(8,128)(2,1)S(1)} %pad_maximum_fusion.refs_0_), channel_id=1, source_target_pairs={{0,1},{1,0},{2,3},{3,2},{4,5},{5,4},{6,7},{7,6},{8,9},{9,8},{10,11... | collective-permute-start | bytes 786440 | tf_op jit(solution)/shard_map/ppermute | solution.py:370

commit v5 on v4

--- a/solution.py
+++ b/solution.py
@@ -278,20 +278,23 @@
                 all_ref[chunk, m * 2 * size : (m + 1) * 2 * size, :] = ref[m, j].astype(jnp.float32)
     n_row, n_col = rows // width, cols // width
     lane = lax.broadcasted_iota(jnp.int32, (width, depth), 1)
-    for q in range(n_row):
-        turned = (all_ref[lax.axis_index("row") * n_row + q] * (1.0 / frames)).T
-        for c in range(cg):
-            mine = jnp.where(lax.rem(lane, cg) == c, turned, 0.0)
+    turned = [(all_ref[lax.axis_index("row") * n_row + q] * (1.0 / frames)).T for q in range(n_row)]
+
+    def set_left(c):
+        for q in range(n_row):
+            mine = jnp.where(lax.rem(lane, cg) == c, turned[q], 0.0)
             left_ref[c, q * width : (q + 1) * width, :] = mine.astype(jnp.bfloat16)
+
     shift = {None: 0, 0: core, 1: 1 - core}[phase]
     first = lax.axis_index("tm") * (out_ref.shape[3] // width) + shift
     low = lax.rem(lax.broadcasted_iota(jnp.int32, (depth, width), 0), size) < cg
-    for q in range(n_col):
-        x = all_ref[first + q]
-        part = slice(q * width, (q + 1) * width)
-        right_ref[0, :, part] = x.astype(jnp.bfloat16)
-        crossed = jnp.where(low, -pltpu.roll(x, depth - cg, 0), pltpu.roll(x, cg, 0))
-        right_ref[1, :, part] = crossed.astype(jnp.bfloat16)
+
+    def set_right(ri):
+        for q in range(n_col):
+            x = all_ref[first + q]
+            if ri == 1:
+                x = jnp.where(low, -pltpu.roll(x, depth - cg, 0), pltpu.roll(x, cg, 0))
+            right_ref[ri, :, q * width : (q + 1) * width] = x.astype(jnp.bfloat16)
 
     high, wide = min(tile, rows), min(tile, cols)
     spots = [(top, left) for left in range(0, cols, wide) for top in range(0, rows, high)]
@@ -313,7 +316,10 @@
                 for s in range(len(spots)):
                     copy(ri, c - slots, s).wait()
 
+        set_left(c)
         for ri in range(2):
+            if c == 0:
+                set_right(ri)
             for s, (top, left) in enumerate(spots):
                 product = jnp.dot(
                     left_ref[c, top : top + high, :],

time: 39.4 us -> 39.4 us (level)
  no operation moved by 1% of the time
where the time goes in v5:
time: 39.4 us; the launch traced here: 39.2 us
  Pallas kernels  17 us (43%)
  starting transfers between devices  13.6 us (35%)
  waiting for transfers between devices  8.33 us (21%)
    pallas_call x2, Pallas kernels, correlate(): pl.pallas_call(functools.partial(correlate_body, phase=phase, tile=TILE),...  12.7 us
    ppermute x2, starting transfers between devices, turn_plane(): return lax.ppermute(value, ('chan', 'row'), pairs)  4.67 us
    ppermute x2, starting transfers between devices, rotated(): lax.ppermute(value, axis, [(i, (i + by) % peers) for i in range(peers)])  4.41 us
    pallas_call x1, Pallas kernels, front(): pl.pallas_call(functools.partial(front_body, groups=groups), name='front'...  4.21 us
    ppermute x3, waiting for transfers between devices, local(): lax.ppermute(pieces, FRAME_AXES, [(i, i ^ 2 * s) for i in range(peers)])  4.03 us
    ppermute x3, starting transfers between devices, local(): lax.ppermute(pieces, FRAME_AXES, [(i, i ^ 2 * s) for i in range(peers)])  3.55 us
    ppermute x2, waiting for transfers between devices, rotated(): lax.ppermute(value, axis, [(i, (i + by) % peers) for i in range(peers)])  2.55 us
    ppermute x2, waiting for transfers between devices, swapped(): return lax.ppermute(value, FRAME_AXES, [(i, i ^ 1) for i in range(peers)])  0.99 us
  transfers between devices with their start and end apart: 9, of which 6 were waited for; matrix products, arithmetic and copies ran while one was open for 0% of the time, Pallas kernels for 16%

profile of v5, /device:TPU:0, one launch (start us, length us, event | category | flops | bytes accessed | tf_op | source)
XLA Modules:
  0.0 39.2 jit_solution(5977713200809375809)
XLA Ops:
  0.0 4.2 %front.1 = (f32[4,16,1024]{2,1,0:T(8,128)S(1)}, bf16[4,16,1024]{2,1,0:T(8,128)(2,1)S(1)}) custom-call(s32[16]{0:T(128)} %index_hbm.1, bf16[1,4096,1024]{2,1,0:T(8,128)(2,1)} %samples_ref.1, f32[16,1024]{1,0:T(8,128)} %gr_hbm.1, f32[16,1024]{1,0:T(8,128)} %gi_hbm.1, s32[1,512]{1,0:T(1,128)} %bitcast.13), custom_call_target="tpu_custom_call" | custom-call | tf_op jit(solution)/shard_map/front/pallas_call | solution.py:176
  4.2 0.6 %collective-permute-start = (bf16[4,16,1024]{2,1,0:T(8,128)(2,1)S(1)}, bf16[4,16,1024]{2,1,0:T(8,128)(2,1)S(1)}, u32[]{:S(2)}, u32[]{:S(2)}) collective-permute-start(bf16[4,16,1024]{2,1,0:T(8,128)(2,1)S(1)} %get-tuple-element.13), channel_id=1, source_target_pairs={{0,1},{1,0},{2,3},{3,2},{4,5},{5,4},{6,7},{7,6},{8,9},{9,8},{10,11... | collective-permute-start | bytes 393224 | tf_op jit(solution)/shard_map/ppermute | solution.py:376
  4.8 1.0 %collective-permute-done.got_ref = bf16[4,16,1024]{2,1,0:T(8,128)(2,1)S(1)} collective-permute-done((bf16[4,16,1024]{2,1,0:T(8,128)(2,1)S(1)}, bf16[4,16,1024]{2,1,0:T(8,128)(2,1)S(1)}, u32[]{:S(2)}, u32[]{:S(2)}) %collective-permute-start) | collective-permute-done | bytes 131104 | tf_op jit(solution)/shard_map/ppermute | solution.py:376
  5.8 2.9 %collective-permute-start.1 = (bf16[32,1024]{1,0:T(8,128)(2,1)S(1)}, bf16[32,1024]{1,0:T(8,128)(2,1)S(1)}, u32[]{:S(2)}, u32[]{:S(2)}) collective-permute-start(bf16[32,1024]{1,0:T(8,128)(2,1)S(1)} %get-tuple-element.15), channel_id=1, source_target_pairs={{0,2},{1,3},{2,4},{3,5},{4,6},{5,7},{6,0},{7,1},{8,10},{9,11},{10,... | collective-permute-start | bytes 196616 | tf_op jit(solution)/shard_map/ppermute | solution.py:29
  8.7 1.5 %collective-permute-start.2 = (bf16[16,1024]{1,0:T(8,128)(2,1)S(1)}, bf16[16,1024]{1,0:T(8,128)(2,1)S(1)}, u32[]{:S(2)}, u32[]{:S(2)}) collective-permute-start(bf16[16,1024]{1,0:T(8,128)(2,1)S(1)} %get-tuple-element.16), channel_id=1, source_target_pairs={{0,4},{1,5},{2,6},{3,7},{4,0},{5,1},{6,2},{7,3},{8,12},{9,13},{10,... | collective-permute-start | bytes 98312 | tf_op jit(solution)/shard_map/ppermute | solution.py:29
  10.2 2.5 %collective-permute-done.2.after_ref = bf16[16,1024]{1,0:T(8,128)(2,1)S(1)} collective-permute-done((bf16[16,1024]{1,0:T(8,128)(2,1)S(1)}, bf16[16,1024]{1,0:T(8,128)(2,1)S(1)}, u32[]{:S(2)}, u32[]{:S(2)}) %collective-permute-start.2) | collective-permute-done | bytes 32800 | tf_op jit(solution)/shard_map/ppermute | solution.py:29
  12.8 0.0 collective-permute-done.1.next_ref
  12.8 3.8 %collective-permute-start.3 = (bf16[16,1024]{1,0:T(8,128)(2,1)S(1)}, bf16[16,1024]{1,0:T(8,128)(2,1)S(1)}, u32[]{:S(2)}, u32[]{:S(2)}) collective-permute-start(bf16[16,1024]{1,0:T(8,128)(2,1)S(1)} %get-tuple-element.17), channel_id=1, source_target_pairs={{0,24},{1,16},{2,26},{3,18},{8,17},{9,25},{10,19},{11,27},{16,8},{... | collective-permute-start | bytes 98312 | tf_op jit(solution)/shard_map/ppermute | solution.py:371
  16.7 0.8 %collective-permute-start.4 = (bf16[16,1024]{1,0:T(8,128)(2,1)S(1)}, bf16[16,1024]{1,0:T(8,128)(2,1)S(1)}, u32[]{:S(2)}, u32[]{:S(2)}) collective-permute-start(bf16[16,1024]{1,0:T(8,128)(2,1)S(1)} %get-tuple-element.18), channel_id=1, source_target_pairs={{0,0},{1,8},{2,2},{3,10},{8,9},{9,1},{10,11},{11,3},{16,16},{17,24... | collective-permute-start | bytes 98312 | tf_op jit(solution)/shard_map/ppermute | solution.py:371
  17.5 0.8 %collective-permute-done.3 = bf16[16,1024]{1,0:T(8,128)(2,1)S(1)} collective-permute-done((bf16[16,1024]{1,0:T(8,128)(2,1)S(1)}, bf16[16,1024]{1,0:T(8,128)(2,1)S(1)}, u32[]{:S(2)}, u32[]{:S(2)}) %collective-permute-start.3) | collective-permute-done | bytes 32800 | tf_op jit(solution)/shard_map/ppermute | solution.py:371
  18.3 0.0 collective-permute-done.4
  18.3 1.6 %collective-permute-start.6 = (bf16[2,16,1024]{2,1,0:T(8,128)(2,1)S(1)}, bf16[2,16,1024]{2,1,0:T(8,128)(2,1)S(1)}, u32[]{:S(2)}, u32[]{:S(2)}) collective-permute-start(bf16[2,16,1024]{2,1,0:T(8,128)(2,1)S(1)} %get-tuple-element.20), channel_id=1, source_target_pairs={{0,4},{1,5},{2,6},{3,7},{4,0},{5,1},{6,2},{7,3},{8,12},{9,13},{10,... | collective-permute-start | bytes 196616 | tf_op jit(solution)/shard_map/ppermute | solution.py:390
  19.9 0.1 collective-permute-start.5
  20.0 1.8 %collective-permute-start.7 = (bf16[2,16,1024]{2,1,0:T(8,128)(2,1)S(1)}, bf16[2,16,1024]{2,1,0:T(8,128)(2,1)S(1)}, u32[]{:S(2)}, u32[]{:S(2)}) collective-permute-start(bf16[2,16,1024]{2,1,0:T(8,128)(2,1)S(1)} %get-tuple-element.20), channel_id=1, source_target_pairs={{0,6},{1,7},{2,4},{3,5},{4,2},{5,3},{6,0},{7,1},{8,14},{9,15},{10,... | collective-permute-start | bytes 196616 | tf_op jit(solution)/shard_map/ppermute | solution.py:390
  21.8 0.8 %collective-permute-done.6 = bf16[2,16,1024]{2,1,0:T(8,128)(2,1)S(1)} collective-permute-done((bf16[2,16,1024]{2,1,0:T(8,128)(2,1)S(1)}, bf16[2,16,1024]{2,1,0:T(8,128)(2,1)S(1)}, u32[]{:S(2)}, u32[]{:S(2)}) %collective-permute-start.6) | collective-permute-done | bytes 65568 | tf_op jit(solution)/shard_map/ppermute | solution.py:390
  22.6 1.5 %collective-permute-done.5 = bf16[2,16,1024]{2,1,0:T(8,128)(2,1)S(1)} collective-permute-done((bf16[2,16,1024]{2,1,0:T(8,128)(2,1)S(1)}, bf16[2,16,1024]{2,1,0:T(8,128)(2,1)S(1)}, u32[]{:S(2)}, u32[]{:S(2)}) %collective-permute-start.5) | collective-permute-done | bytes 65568 | tf_op jit(solution)/shard_map/ppermute | solution.py:390
  24.1 1.7 %collective-permute-done.7 = bf16[2,16,1024]{2,1,0:T(8,128)(2,1)S(1)} collective-permute-done((bf16[2,16,1024]{2,1,0:T(8,128)(2,1)S(1)}, bf16[2,16,1024]{2,1,0:T(8,128)(2,1)S(1)}, u32[]{:S(2)}, u32[]{:S(2)}) %collective-permute-start.7) | collective-permute-done | bytes 65568 | tf_op jit(solution)/shard_map/ppermute | solution.py:390
  25.9 0.4 %collective-permute-start.8 = (bf16[4,2,16,1024]{3,2,1,0:T(8,128)(2,1)S(1)}, bf16[4,2,16,1024]{3,2,1,0:T(8,128)(2,1)S(1)}, u32[]{:S(2)}, u32[]{:S(2)}) collective-permute-start(bf16[4,2,16,1024]{3,2,1,0:T(8,128)(2,1)S(1)} %pad_maximum_fusion.refs_0_), channel_id=1, source_target_pairs={{0,1},{1,0},{2,3},{3,2},{4,5},{5,4},{6,7},{7,6},{8,9},{9,8},{10,11... | collective-permute-start | bytes 786440 | tf_op jit(solution)/shard_map/ppermute | solution.py:376
  26.3 6.3 %correlate_near.1.refs_2_ = bf16[2,4,1024,2048]{3,2,1,0:T(8,128)(2,1)} custom-call(bf16[4,2,16,1024]{3,2,1,0:T(8,128)(2,1)S(1)} %pad_maximum_fusion.refs_0_), custom_call_target="tpu_custom_call" | custom-call | tf_op jit(solution)/shard_map/correlate_near/pallas_call | solution.py:346
  32.6 0.0 collective-permute-done.8.refs_1_
  32.7 6.4 %correlate_far.1 = bf16[2,4,1024,2048]{3,2,1,0:T(8,128)(2,1)} custom-call(bf16[4,2,16,1024]{3,2,1,0:T(8,128)(2,1)S(1)} %pad_maximum_fusion.refs_0_, bf16[4,2,16,1024]{3,2,1,0:T(8,128)(2,1)S(1)} %collective-permute-done.8.refs_1_, bf16[2,4,1024,2048]{3,2,1,0:T(8,128)(2,1)} %correlate_near.1.refs_2_), custom_call_target="tpu_custom_call", output_to_operand_aliasing={{}: (2, {})} | custom-call | tf_op jit(solution)/shard_map/correlate_far/pallas_call | solution.py:346
  (4 shorter events, 0.1 us)
Async XLA Ops:
  4.2 1.5 %collective-permute-start = (bf16[4,16,1024]{2,1,0:T(8,128)(2,1)S(1)}, bf16[4,16,1024]{2,1,0:T(8,128)(2,1)S(1)}, u32[]{:S(2)}, u32[]{:S(2)}) collective-permute-start(bf16[4,16,1024]{2,1,0:T(8,128)(2,1)S(1)} %get-tuple-element.13), channel_id=1, source_target_pairs={{0,1},{1,0},{2,3},{3,2},{4,5},{5,4},{6,7},{7,6},{8,9},{9,8},{10,11... | collective-permute-start | bytes 393224 | tf_op jit(solution)/shard_map/ppermute | solution.py:376
  5.8 7.0 %collective-permute-start.1 = (bf16[32,1024]{1,0:T(8,128)(2,1)S(1)}, bf16[32,1024]{1,0:T(8,128)(2,1)S(1)}, u32[]{:S(2)}, u32[]{:S(2)}) collective-permute-start(bf16[32,1024]{1,0:T(8,128)(2,1)S(1)} %get-tuple-element.15), channel_id=1, source_target_pairs={{0,2},{1,3},{2,4},{3,5},{4,6},{5,7},{6,0},{7,1},{8,10},{9,11},{10,... | collective-permute-start | bytes 196616 | tf_op jit(solution)/shard_map/ppermute | solution.py:29
  8.7 4.1 %collective-permute-start.2 = (bf16[16,1024]{1,0:T(8,128)(2,1)S(1)}, bf16[16,1024]{1,0:T(8,128)(2,1)S(1)}, u32[]{:S(2)}, u32[]{:S(2)}) collective-permute-start(bf16[16,1024]{1,0:T(8,128)(2,1)S(1)} %get-tuple-element.16), channel_id=1, source_target_pairs={{0,4},{1,5},{2,6},{3,7},{4,0},{5,1},{6,2},{7,3},{8,12},{9,13},{10,... | collective-permute-start | bytes 98312 | tf_op jit(solution)/shard_map/ppermute | solution.py:29
  12.8 5.4 %collective-permute-start.3 = (bf16[16,1024]{1,0:T(8,128)(2,1)S(1)}, bf16[16,1024]{1,0:T(8,128)(2,1)S(1)}, u32[]{:S(2)}, u32[]{:S(2)}) collective-permute-start(bf16[16,1024]{1,0:T(8,128)(2,1)S(1)} %get-tuple-element.17), channel_id=1, source_target_pairs={{0,24},{1,16},{2,26},{3,18},{8,17},{9,25},{10,19},{11,27},{16,8},{... | collective-permute-start | bytes 98312 | tf_op jit(solution)/shard_map/ppermute | solution.py:371
  16.7 1.6 %collective-permute-start.4 = (bf16[16,1024]{1,0:T(8,128)(2,1)S(1)}, bf16[16,1024]{1,0:T(8,128)(2,1)S(1)}, u32[]{:S(2)}, u32[]{:S(2)}) collective-permute-start(bf16[16,1024]{1,0:T(8,128)(2,1)S(1)} %get-tuple-element.18), channel_id=1, source_target_pairs={{0,0},{1,8},{2,2},{3,10},{8,9},{9,1},{10,11},{11,3},{16,16},{17,24... | collective-permute-start | bytes 98312 | tf_op jit(solution)/shard_map/ppermute | solution.py:371
  18.3 4.3 %collective-permute-start.6 = (bf16[2,16,1024]{2,1,0:T(8,128)(2,1)S(1)}, bf16[2,16,1024]{2,1,0:T(8,128)(2,1)S(1)}, u32[]{:S(2)}, u32[]{:S(2)}) collective-permute-start(bf16[2,16,1024]{2,1,0:T(8,128)(2,1)S(1)} %get-tuple-element.20), channel_id=1, source_target_pairs={{0,4},{1,5},{2,6},{3,7},{4,0},{5,1},{6,2},{7,3},{8,12},{9,13},{10,... | collective-permute-start | bytes 196616 | tf_op jit(solution)/shard_map/ppermute | solution.py:390
  19.9 4.3 %collective-permute-start.5 = (bf16[2,16,1024]{2,1,0:T(8,128)(2,1)S(1)}, bf16[2,16,1024]{2,1,0:T(8,128)(2,1)S(1)}, u32[]{:S(2)}, u32[]{:S(2)}) collective-permute-start(bf16[2,16,1024]{2,1,0:T(8,128)(2,1)S(1)} %get-tuple-element.20), channel_id=1, source_target_pairs={{0,2},{1,3},{2,0},{3,1},{4,6},{5,7},{6,4},{7,5},{8,10},{9,11},{10,... | collective-permute-start | bytes 196616 | tf_op jit(solution)/shard_map/ppermute | solution.py:390
  20.0 5.9 %collective-permute-start.7 = (bf16[2,16,1024]{2,1,0:T(8,128)(2,1)S(1)}, bf16[2,16,1024]{2,1,0:T(8,128)(2,1)S(1)}, u32[]{:S(2)}, u32[]{:S(2)}) collective-permute-start(bf16[2,16,1024]{2,1,0:T(8,128)(2,1)S(1)} %get-tuple-element.20), channel_id=1, source_target_pairs={{0,6},{1,7},{2,4},{3,5},{4,2},{5,3},{6,0},{7,1},{8,14},{9,15},{10,... | collective-permute-start | bytes 196616 | tf_op jit(solution)/shard_map/ppermute | solution.py:390
  25.9 6.7 %collective-permute-start.8 = (bf16[4,2,16,1024]{3,2,1,0:T(8,128)(2,1)S(1)}, bf16[4,2,16,1024]{3,2,1,0:T(8,128)(2,1)S(1)}, u32[]{:S(2)}, u32[]{:S(2)}) collective-permute-start(bf16[4,2,16,1024]{3,2,1,0:T(8,128)(2,1)S(1)} %pad_maximum_fusion.refs_0_), channel_id=1, source_target_pairs={{0,1},{1,0},{2,3},{3,2},{4,5},{5,4},{6,7},{7,6},{8,9},{9,8},{10,11... | collective-permute-start | bytes 786440 | tf_op jit(solution)/shard_map/ppermute | solution.py:376

commit v6 on v5

--- a/solution.py
+++ b/solution.py
@@ -11,7 +11,7 @@
 TAPS = 4
 LANES = 128
 PAIR_TAPS = (1, 2)
-SPLITS = 8
+SHARES = (3, 3, 3, 3, 2, 1, 1)
 TILE = 512
 VMEM_BYTES = 48 << 20
 FRAME_AXES = ("tm", "row")
@@ -75,12 +75,13 @@
     quarter = points // 4
     index_copy = pltpu.make_async_copy(index_hbm, index_ref, small_sems.at[0])
     index_copy.start()
-    part = points // SPLITS
+    edges = [points * sum(SHARES[:i]) // sum(SHARES) for i in range(len(SHARES) + 1)]
+    pieces = list(zip(edges, edges[1:]))
     fetches = [
         pltpu.make_async_copy(
-            samples_ref.at[0, pl.ds(i * part, part), :], block_ref.at[pl.ds(i * part, part), :], sems.at[i]
+            samples_ref.at[0, pl.ds(lo, hi - lo), :], block_ref.at[pl.ds(lo, hi - lo), :], sems.at[i]
         )
-        for i in range(SPLITS)
+        for i, (lo, hi) in enumerate(pieces)
     ]
     for copy in fetches:
         copy.start()
@@ -125,7 +126,7 @@
                 table_ref[i * rows : (i + 1) * rows, cols] = (t - high.astype(jnp.float32)).astype(jnp.bfloat16)
     for i, copy in enumerate(fetches):
         copy.wait()
-        span = slice(i * part, (i + 1) * part)
+        span = slice(*pieces[i])
         product = jnp.dot(table_ref[:, span], block_ref[span, :], preferred_element_type=jnp.float32)
         acc_ref[...] = product if i == 0 else acc_ref[...] + product
 
@@ -192,7 +193,7 @@
             pltpu.VMEM((depth, points), jnp.bfloat16),
             pltpu.VMEM((depth, width), jnp.float32),
             pltpu.VMEM((groups, rows // groups, width), jnp.float32),
-            pltpu.SemaphoreType.DMA((SPLITS,)),
+            pltpu.SemaphoreType.DMA((len(SHARES),)),
             pltpu.SemaphoreType.DMA((4,)),
         ],
         compiler_params=pltpu.CompilerParams(vmem_limit_bytes=VMEM_BYTES),

time: 39.4 us -> 39.4 us (level)
  no operation moved by 1% of the time
where the time goes in v6:
time: 39.4 us; the launch traced here: 39.3 us
  Pallas kernels  17.1 us (43%)
  starting transfers between devices  13.6 us (35%)
  waiting for transfers between devices  8.33 us (21%)
    pallas_call x2, Pallas kernels, correlate(): pl.pallas_call(functools.partial(correlate_body, phase=phase, tile=TILE),...  12.7 us
    ppermute x2, starting transfers between devices, turn_plane(): return lax.ppermute(value, ('chan', 'row'), pairs)  4.67 us
    ppermute x2, starting transfers between devices, rotated(): lax.ppermute(value, axis, [(i, (i + by) % peers) for i in range(peers)])  4.41 us
    pallas_call x1, Pallas kernels, front(): pl.pallas_call(functools.partial(front_body, groups=groups), name='front'...  4.27 us
    ppermute x3, waiting for transfers between devices, local(): lax.ppermute(pieces, FRAME_AXES, [(i, i ^ 2 * s) for i in range(peers)])  4.03 us
    ppermute x3, starting transfers between devices, local(): lax.ppermute(pieces, FRAME_AXES, [(i, i ^ 2 * s) for i in range(peers)])  3.55 us
    ppermute x2, waiting for transfers between devices, rotated(): lax.ppermute(value, axis, [(i, (i + by) % peers) for i in range(peers)])  2.55 us
    ppermute x2, waiting for transfers between devices, swapped(): return lax.ppermute(value, FRAME_AXES, [(i, i ^ 1) for i in range(peers)])  0.99 us
  transfers between devices with their start and end apart: 9, of which 6 were waited for; matrix products, arithmetic and copies ran while one was open for 0% of the time, Pallas kernels for 16%

profile of v6, /device:TPU:0, one launch (start us, length us, event | category | flops | bytes accessed | tf_op | source)
XLA Modules:
  0.0 39.3 jit_solution(16086844818947623017)
XLA Ops:
  0.0 4.3 %front.1 = (f32[4,16,1024]{2,1,0:T(8,128)S(1)}, bf16[4,16,1024]{2,1,0:T(8,128)(2,1)S(1)}) custom-call(s32[16]{0:T(128)} %index_hbm.1, bf16[1,4096,1024]{2,1,0:T(8,128)(2,1)} %samples_ref.1, f32[16,1024]{1,0:T(8,128)} %gr_hbm.1, f32[16,1024]{1,0:T(8,128)} %gi_hbm.1, s32[1,512]{1,0:T(1,128)} %bitcast.13), custom_call_target="tpu_custom_call" | custom-call | tf_op jit(solution)/shard_map/front/pallas_call | solution.py:177
  4.3 0.6 %collective-permute-start = (bf16[4,16,1024]{2,1,0:T(8,128)(2,1)S(1)}, bf16[4,16,1024]{2,1,0:T(8,128)(2,1)S(1)}, u32[]{:S(2)}, u32[]{:S(2)}) collective-permute-start(bf16[4,16,1024]{2,1,0:T(8,128)(2,1)S(1)} %get-tuple-element.13), channel_id=1, source_target_pairs={{0,1},{1,0},{2,3},{3,2},{4,5},{5,4},{6,7},{7,6},{8,9},{9,8},{10,11... | collective-permute-start | bytes 393224 | tf_op jit(solution)/shard_map/ppermute | solution.py:377
  4.8 1.0 %collective-permute-done.got_ref = bf16[4,16,1024]{2,1,0:T(8,128)(2,1)S(1)} collective-permute-done((bf16[4,16,1024]{2,1,0:T(8,128)(2,1)S(1)}, bf16[4,16,1024]{2,1,0:T(8,128)(2,1)S(1)}, u32[]{:S(2)}, u32[]{:S(2)}) %collective-permute-start) | collective-permute-done | bytes 131104 | tf_op jit(solution)/shard_map/ppermute | solution.py:377
  5.9 2.9 %collective-permute-start.1 = (bf16[32,1024]{1,0:T(8,128)(2,1)S(1)}, bf16[32,1024]{1,0:T(8,128)(2,1)S(1)}, u32[]{:S(2)}, u32[]{:S(2)}) collective-permute-start(bf16[32,1024]{1,0:T(8,128)(2,1)S(1)} %get-tuple-element.15), channel_id=1, source_target_pairs={{0,2},{1,3},{2,4},{3,5},{4,6},{5,7},{6,0},{7,1},{8,10},{9,11},{10,... | collective-permute-start | bytes 196616 | tf_op jit(solution)/shard_map/ppermute | solution.py:29
  8.8 1.5 %collective-permute-start.2 = (bf16[16,1024]{1,0:T(8,128)(2,1)S(1)}, bf16[16,1024]{1,0:T(8,128)(2,1)S(1)}, u32[]{:S(2)}, u32[]{:S(2)}) collective-permute-start(bf16[16,1024]{1,0:T(8,128)(2,1)S(1)} %get-tuple-element.16), channel_id=1, source_target_pairs={{0,4},{1,5},{2,6},{3,7},{4,0},{5,1},{6,2},{7,3},{8,12},{9,13},{10,... | collective-permute-start | bytes 98312 | tf_op jit(solution)/shard_map/ppermute | solution.py:29
  10.3 2.5 %collective-permute-done.2.after_ref = bf16[16,1024]{1,0:T(8,128)(2,1)S(1)} collective-permute-done((bf16[16,1024]{1,0:T(8,128)(2,1)S(1)}, bf16[16,1024]{1,0:T(8,128)(2,1)S(1)}, u32[]{:S(2)}, u32[]{:S(2)}) %collective-permute-start.2) | collective-permute-done | bytes 32800 | tf_op jit(solution)/shard_map/ppermute | solution.py:29
  12.8 0.0 collective-permute-done.1.next_ref
  12.9 3.8 %collective-permute-start.3 = (bf16[16,1024]{1,0:T(8,128)(2,1)S(1)}, bf16[16,1024]{1,0:T(8,128)(2,1)S(1)}, u32[]{:S(2)}, u32[]{:S(2)}) collective-permute-start(bf16[16,1024]{1,0:T(8,128)(2,1)S(1)} %get-tuple-element.17), channel_id=1, source_target_pairs={{0,24},{1,16},{2,26},{3,18},{8,17},{9,25},{10,19},{11,27},{16,8},{... | collective-permute-start | bytes 98312 | tf_op jit(solution)/shard_map/ppermute | solution.py:372
  16.7 0.8 %collective-permute-start.4 = (bf16[16,1024]{1,0:T(8,128)(2,1)S(1)}, bf16[16,1024]{1,0:T(8,128)(2,1)S(1)}, u32[]{:S(2)}, u32[]{:S(2)}) collective-permute-start(bf16[16,1024]{1,0:T(8,128)(2,1)S(1)} %get-tuple-element.18), channel_id=1, source_target_pairs={{0,0},{1,8},{2,2},{3,10},{8,9},{9,1},{10,11},{11,3},{16,16},{17,24... | collective-permute-start | bytes 98312 | tf_op jit(solution)/shard_map/ppermute | solution.py:372
  17.6 0.8 %collective-permute-done.3 = bf16[16,1024]{1,0:T(8,128)(2,1)S(1)} collective-permute-done((bf16[16,1024]{1,0:T(8,128)(2,1)S(1)}, bf16[16,1024]{1,0:T(8,128)(2,1)S(1)}, u32[]{:S(2)}, u32[]{:S(2)}) %collective-permute-start.3) | collective-permute-done | bytes 32800 | tf_op jit(solution)/shard_map/ppermute | solution.py:372
  18.3 0.0 collective-permute-done.4
  18.3 1.6 %collective-permute-start.6 = (bf16[2,16,1024]{2,1,0:T(8,128)(2,1)S(1)}, bf16[2,16,1024]{2,1,0:T(8,128)(2,1)S(1)}, u32[]{:S(2)}, u32[]{:S(2)}) collective-permute-start(bf16[2,16,1024]{2,1,0:T(8,128)(2,1)S(1)} %get-tuple-element.20), channel_id=1, source_target_pairs={{0,4},{1,5},{2,6},{3,7},{4,0},{5,1},{6,2},{7,3},{8,12},{9,13},{10,... | collective-permute-start | bytes 196616 | tf_op jit(solution)/shard_map/ppermute | solution.py:391
  19.9 0.1 collective-permute-start.5
  20.1 1.8 %collective-permute-start.7 = (bf16[2,16,1024]{2,1,0:T(8,128)(2,1)S(1)}, bf16[2,16,1024]{2,1,0:T(8,128)(2,1)S(1)}, u32[]{:S(2)}, u32[]{:S(2)}) collective-permute-start(bf16[2,16,1024]{2,1,0:T(8,128)(2,1)S(1)} %get-tuple-element.20), channel_id=1, source_target_pairs={{0,6},{1,7},{2,4},{3,5},{4,2},{5,3},{6,0},{7,1},{8,14},{9,15},{10,... | collective-permute-start | bytes 196616 | tf_op jit(solution)/shard_map/ppermute | solution.py:391
  21.9 0.8 %collective-permute-done.6 = bf16[2,16,1024]{2,1,0:T(8,128)(2,1)S(1)} collective-permute-done((bf16[2,16,1024]{2,1,0:T(8,128)(2,1)S(1)}, bf16[2,16,1024]{2,1,0:T(8,128)(2,1)S(1)}, u32[]{:S(2)}, u32[]{:S(2)}) %collective-permute-start.6) | collective-permute-done | bytes 65568 | tf_op jit(solution)/shard_map/ppermute | solution.py:391
  22.7 1.5 %collective-permute-done.5 = bf16[2,16,1024]{2,1,0:T(8,128)(2,1)S(1)} collective-permute-done((bf16[2,16,1024]{2,1,0:T(8,128)(2,1)S(1)}, bf16[2,16,1024]{2,1,0:T(8,128)(2,1)S(1)}, u32[]{:S(2)}, u32[]{:S(2)}) %collective-permute-start.5) | collective-permute-done | bytes 65568 | tf_op jit(solution)/shard_map/ppermute | solution.py:391
  24.2 1.7 %collective-permute-done.7 = bf16[2,16,1024]{2,1,0:T(8,128)(2,1)S(1)} collective-permute-done((bf16[2,16,1024]{2,1,0:T(8,128)(2,1)S(1)}, bf16[2,16,1024]{2,1,0:T(8,128)(2,1)S(1)}, u32[]{:S(2)}, u32[]{:S(2)}) %collective-permute-start.7) | collective-permute-done | bytes 65568 | tf_op jit(solution)/shard_map/ppermute | solution.py:391
  26.0 0.4 %collective-permute-start.8 = (bf16[4,2,16,1024]{3,2,1,0:T(8,128)(2,1)S(1)}, bf16[4,2,16,1024]{3,2,1,0:T(8,128)(2,1)S(1)}, u32[]{:S(2)}, u32[]{:S(2)}) collective-permute-start(bf16[4,2,16,1024]{3,2,1,0:T(8,128)(2,1)S(1)} %pad_maximum_fusion.refs_0_), channel_id=1, source_target_pairs={{0,1},{1,0},{2,3},{3,2},{4,5},{5,4},{6,7},{7,6},{8,9},{9,8},{10,11... | collective-permute-start | bytes 786440 | tf_op jit(solution)/shard_map/ppermute | solution.py:377
  26.4 6.3 %correlate_near.1.refs_2_ = bf16[2,4,1024,2048]{3,2,1,0:T(8,128)(2,1)} custom-call(bf16[4,2,16,1024]{3,2,1,0:T(8,128)(2,1)S(1)} %pad_maximum_fusion.refs_0_), custom_call_target="tpu_custom_call" | custom-call | tf_op jit(solution)/shard_map/correlate_near/pallas_call | solution.py:347
  32.7 0.0 collective-permute-done.8.refs_1_
  32.7 6.4 %correlate_far.1 = bf16[2,4,1024,2048]{3,2,1,0:T(8,128)(2,1)} custom-call(bf16[4,2,16,1024]{3,2,1,0:T(8,128)(2,1)S(1)} %pad_maximum_fusion.refs_0_, bf16[4,2,16,1024]{3,2,1,0:T(8,128)(2,1)S(1)} %collective-permute-done.8.refs_1_, bf16[2,4,1024,2048]{3,2,1,0:T(8,128)(2,1)} %correlate_near.1.refs_2_), custom_call_target="tpu_custom_call", output_to_operand_aliasing={{}: (2, {})} | custom-call | tf_op jit(solution)/shard_map/correlate_far/pallas_call | solution.py:347
  (4 shorter events, 0.1 us)
Async XLA Ops:
  4.3 1.5 %collective-permute-start = (bf16[4,16,1024]{2,1,0:T(8,128)(2,1)S(1)}, bf16[4,16,1024]{2,1,0:T(8,128)(2,1)S(1)}, u32[]{:S(2)}, u32[]{:S(2)}) collective-permute-start(bf16[4,16,1024]{2,1,0:T(8,128)(2,1)S(1)} %get-tuple-element.13), channel_id=1, source_target_pairs={{0,1},{1,0},{2,3},{3,2},{4,5},{5,4},{6,7},{7,6},{8,9},{9,8},{10,11... | collective-permute-start | bytes 393224 | tf_op jit(solution)/shard_map/ppermute | solution.py:377
  5.9 7.0 %collective-permute-start.1 = (bf16[32,1024]{1,0:T(8,128)(2,1)S(1)}, bf16[32,1024]{1,0:T(8,128)(2,1)S(1)}, u32[]{:S(2)}, u32[]{:S(2)}) collective-permute-start(bf16[32,1024]{1,0:T(8,128)(2,1)S(1)} %get-tuple-element.15), channel_id=1, source_target_pairs={{0,2},{1,3},{2,4},{3,5},{4,6},{5,7},{6,0},{7,1},{8,10},{9,11},{10,... | collective-permute-start | bytes 196616 | tf_op jit(solution)/shard_map/ppermute | solution.py:29
  8.8 4.1 %collective-permute-start.2 = (bf16[16,1024]{1,0:T(8,128)(2,1)S(1)}, bf16[16,1024]{1,0:T(8,128)(2,1)S(1)}, u32[]{:S(2)}, u32[]{:S(2)}) collective-permute-start(bf16[16,1024]{1,0:T(8,128)(2,1)S(1)} %get-tuple-element.16), channel_id=1, source_target_pairs={{0,4},{1,5},{2,6},{3,7},{4,0},{5,1},{6,2},{7,3},{8,12},{9,13},{10,... | collective-permute-start | bytes 98312 | tf_op jit(solution)/shard_map/ppermute | solution.py:29
  12.9 5.4 %collective-permute-start.3 = (bf16[16,1024]{1,0:T(8,128)(2,1)S(1)}, bf16[16,1024]{1,0:T(8,128)(2,1)S(1)}, u32[]{:S(2)}, u32[]{:S(2)}) collective-permute-start(bf16[16,1024]{1,0:T(8,128)(2,1)S(1)} %get-tuple-element.17), channel_id=1, source_target_pairs={{0,24},{1,16},{2,26},{3,18},{8,17},{9,25},{10,19},{11,27},{16,8},{... | collective-permute-start | bytes 98312 | tf_op jit(solution)/shard_map/ppermute | solution.py:372
  16.7 1.6 %collective-permute-start.4 = (bf16[16,1024]{1,0:T(8,128)(2,1)S(1)}, bf16[16,1024]{1,0:T(8,128)(2,1)S(1)}, u32[]{:S(2)}, u32[]{:S(2)}) collective-permute-start(bf16[16,1024]{1,0:T(8,128)(2,1)S(1)} %get-tuple-element.18), channel_id=1, source_target_pairs={{0,0},{1,8},{2,2},{3,10},{8,9},{9,1},{10,11},{11,3},{16,16},{17,24... | collective-permute-start | bytes 98312 | tf_op jit(solution)/shard_map/ppermute | solution.py:372
  18.3 4.3 %collective-permute-start.6 = (bf16[2,16,1024]{2,1,0:T(8,128)(2,1)S(1)}, bf16[2,16,1024]{2,1,0:T(8,128)(2,1)S(1)}, u32[]{:S(2)}, u32[]{:S(2)}) collective-permute-start(bf16[2,16,1024]{2,1,0:T(8,128)(2,1)S(1)} %get-tuple-element.20), channel_id=1, source_target_pairs={{0,4},{1,5},{2,6},{3,7},{4,0},{5,1},{6,2},{7,3},{8,12},{9,13},{10,... | collective-permute-start | bytes 196616 | tf_op jit(solution)/shard_map/ppermute | solution.py:391
  19.9 4.3 %collective-permute-start.5 = (bf16[2,16,1024]{2,1,0:T(8,128)(2,1)S(1)}, bf16[2,16,1024]{2,1,0:T(8,128)(2,1)S(1)}, u32[]{:S(2)}, u32[]{:S(2)}) collective-permute-start(bf16[2,16,1024]{2,1,0:T(8,128)(2,1)S(1)} %get-tuple-element.20), channel_id=1, source_target_pairs={{0,2},{1,3},{2,0},{3,1},{4,6},{5,7},{6,4},{7,5},{8,10},{9,11},{10,... | collective-permute-start | bytes 196616 | tf_op jit(solution)/shard_map/ppermute | solution.py:391
  20.1 5.9 %collective-permute-start.7 = (bf16[2,16,1024]{2,1,0:T(8,128)(2,1)S(1)}, bf16[2,16,1024]{2,1,0:T(8,128)(2,1)S(1)}, u32[]{:S(2)}, u32[]{:S(2)}) collective-permute-start(bf16[2,16,1024]{2,1,0:T(8,128)(2,1)S(1)} %get-tuple-element.20), channel_id=1, source_target_pairs={{0,6},{1,7},{2,4},{3,5},{4,2},{5,3},{6,0},{7,1},{8,14},{9,15},{10,... | collective-permute-start | bytes 196616 | tf_op jit(solution)/shard_map/ppermute | solution.py:391
  26.0 6.8 %collective-permute-start.8 = (bf16[4,2,16,1024]{3,2,1,0:T(8,128)(2,1)S(1)}, bf16[4,2,16,1024]{3,2,1,0:T(8,128)(2,1)S(1)}, u32[]{:S(2)}, u32[]{:S(2)}) collective-permute-start(bf16[4,2,16,1024]{3,2,1,0:T(8,128)(2,1)S(1)} %pad_maximum_fusion.refs_0_), channel_id=1, source_target_pairs={{0,1},{1,0},{2,3},{3,2},{4,5},{5,4},{6,7},{7,6},{8,9},{9,8},{10,11... | collective-permute-start | bytes 786440 | tf_op jit(solution)/shard_map/ppermute | solution.py:377
